TPU v7x, 1024 devices: a whole 4x8x16 slice. The times are simulated.
1024 devices in a mesh: ctx: 16 (over z_hi, x), exp: 64 (over y, z_lo, core).
Axes of the slice: x: 4, y: 8, z: 16 (z_hi: 4, z_lo: 4; z = z_hi * 4 + z_lo), core: 2. Of those that a mesh axis runs over, the one named last changes fastest.
Arguments:
- query: bfloat16 [64, 2048, 2048], P('exp', 'ctx'), may hold values from -8 to 8
- key_value: bfloat16 [64, 2048, 256], P('exp', 'ctx'), may hold values from -8 to 8
- prior_out: bfloat16 [64, 2048, 2048], P('exp', 'ctx'), may hold values from -6 to 6
- prior_lse: float32 [64, 2048, 32], P('exp', 'ctx'), may hold values from 5 to 9
- norm_gain: float32 [2048], replicated, may hold values from 0.25 to 1.75
- w_gate: bfloat16 [64, 2048, 768], P('exp'), may hold values from -0.125 to 0.125
- w_up: bfloat16 [64, 2048, 768], P('exp'), may hold values from -0.125 to 0.125
- expert_ids: int32 [64, 2048, 2], P('exp', 'ctx'), may hold values from 0 to 63, all different within a row; in each aligned block of 128 rows (0 to 127, 128 to 255, ..., all dimensions but the last counted through in order) at most 6 rows name the same one
- route_weight: bfloat16 [64, 2048, 2], P('exp', 'ctx'), may hold values from 0.099609375 to 1
Outputs:
- attended: bfloat16 [64, 2048, 2048], P('exp', 'ctx')
- expert_hidden: bfloat16 [16, 64, 384, 768], P('ctx', 'exp')
Inputs may be any that keep to these rules, and one draw needn't show every extreme that they name: `expert_ids`: each token names 2 different experts; the rows of one device name one expert at most 6 times, a bound that some block reaches.
All inputs are finite; a program needn't handle non-finite values.
Results may differ from a plain program's by a relative error of at most 0.0072.
Values may be sent and summed in bfloat16 or wider, within the bound.
No kernel may reach another device: no remote copies, remote signals or barrier semaphores. Data moves between devices by JAX's collectives and lax.ppermute only.
A program may use at most 64 MiB of HBM per device.

v0:
```python
import jax
import jax.numpy as jnp
from jax import lax
from jax.sharding import PartitionSpec as P

HQ = 32
KVH = 2
HD = 64
FF = 768
STEPS = 3
IN_FLIGHT = 2


def passed_along(block, axis, distance):
    devices = range(lax.axis_size(axis))
    route = [((i - distance) % len(devices), i) for i in devices]
    return lax.ppermute(block, axis, route)


def folded_positions(block_index, row_count, block_total):
    offset = jnp.arange(row_count, dtype=jnp.int32)
    half_rows = row_count // 2
    return jnp.where(
        offset < half_rows,
        block_index * half_rows + offset,
        (2 * block_total - 1 - block_index) * half_rows + offset - half_rows,
    )


def attend_local(queries, window, window_pos, query_pos, prior_rows, prior_logs):
    row_count = queries.shape[0]
    key_count = window.shape[0]
    group_size = HQ // KVH
    grouped = jnp.transpose(queries.reshape(row_count, KVH, group_size, HD), (1, 0, 2, 3))
    grouped = grouped.reshape(KVH, row_count * group_size, HD)
    key_rows = jnp.transpose(window[:, : KVH * HD].reshape(key_count, KVH, HD), (1, 0, 2))
    value_rows = jnp.transpose(window[:, KVH * HD :].reshape(key_count, KVH, HD), (1, 0, 2))
    scores = jnp.einsum(
        "gqd,gsd->gqs", grouped, key_rows, preferred_element_type=jnp.float32
    ) * HD ** (-0.5)
    scores = scores.reshape(KVH, row_count, group_size, key_count)
    allowed = (window_pos[None, :] <= query_pos[:, None])[None, :, None, :]
    scores = jnp.where(allowed, scores, -1e30)
    logs = jnp.transpose(prior_logs.reshape(row_count, KVH, group_size), (1, 0, 2))
    row_max = jnp.maximum(jnp.max(scores, axis=-1), logs)
    powers = jnp.exp(scores - row_max[..., None])
    carried = jnp.exp(logs - row_max)
    denominator = carried + jnp.sum(powers, axis=-1)
    powers_low = powers.astype(jnp.bfloat16).reshape(KVH, row_count * group_size, key_count)
    mixed = jnp.einsum("gqs,gsd->gqd", powers_low, value_rows, preferred_element_type=jnp.float32)
    mixed = mixed.reshape(KVH, row_count, group_size, HD)
    earlier = jnp.transpose(
        prior_rows.reshape(row_count, KVH, group_size, HD), (1, 0, 2, 3)
    ).astype(jnp.float32)
    result = (carried[..., None] * earlier + mixed) / denominator[..., None]
    result = jnp.transpose(result, (1, 0, 2, 3))
    return result.reshape(row_count, HQ * HD).astype(jnp.bfloat16)


def normalize(row_block, gain_row):
    values = row_block.astype(jnp.float32)
    inverse = lax.rsqrt(jnp.mean(values * values, axis=-1, keepdims=True) + 1e-06)
    return (values * inverse * gain_row).astype(jnp.bfloat16)


def slot_sources(ids_flat, expert_total, capacity):
    assign_total = ids_flat.shape[0]
    onehot = (ids_flat[:, None] == jnp.arange(expert_total, dtype=jnp.int32)[None, :]).astype(
        jnp.int32
    )
    before = jnp.cumsum(onehot, axis=0) - onehot
    rank = jnp.sum(before * onehot, axis=1)
    slot_of = ids_flat * capacity + rank
    match = slot_of[None, :] == jnp.arange(expert_total * capacity, dtype=jnp.int32)[:, None]
    numbered = jnp.arange(assign_total, dtype=jnp.int32)[None, :] + 1
    return jnp.sum(jnp.where(match, numbered, 0), axis=1) - 1


def per_device(
    query, key_value, prior_out, prior_lse, norm_gain, w_gate, w_up, expert_ids, route_weight
):
    ctx_total = lax.axis_size("ctx")
    exp_total = lax.axis_size("exp")
    ctx_index = lax.axis_index("ctx")
    row_count = query.shape[1]
    own_pairs = key_value[0]
    blocks = [own_pairs]
    moving = own_pairs
    for step_index in range(1, STEPS):
        moving = passed_along(moving, "ctx", 1)
        blocks.append(moving)
    window = jnp.concatenate(blocks, axis=0)
    sources = (ctx_index - jnp.arange(STEPS, dtype=jnp.int32)) % ctx_total

    def block_positions(block_index):
        return folded_positions(block_index, row_count, ctx_total)

    window_pos = jax.vmap(block_positions)(sources).reshape(-1)
    query_pos = block_positions(ctx_index)
    attended = attend_local(query[0], window, window_pos, query_pos, prior_out[0], prior_lse[0])
    outgoing = normalize(attended, norm_gain)
    capacity = max(2, IN_FLIGHT * row_count * 3 // (2 * exp_total))
    source_of = slot_sources(expert_ids[0].reshape(-1), exp_total, capacity)
    filled = source_of >= 0
    clamped = jnp.maximum(source_of, 0)
    payload = jnp.where(
        filled[:, None], outgoing[clamped // IN_FLIGHT], jnp.zeros((), jnp.bfloat16)
    )
    payload = payload.reshape(exp_total, capacity, HQ * HD)
    slot_weights = jnp.where(
        filled, route_weight[0].reshape(-1)[clamped], jnp.zeros((), jnp.bfloat16)
    )
    slot_weights = slot_weights.reshape(exp_total, capacity)
    arrived_rows, arrived_weights = (
        lax.all_to_all(payload, "exp", split_axis=0, concat_axis=0, tiled=True),
        lax.all_to_all(slot_weights, "exp", split_axis=0, concat_axis=0, tiled=True),
    )
    flat_rows = arrived_rows.reshape(-1, arrived_rows.shape[-1])
    gate_out = jnp.dot(flat_rows, w_gate[0], preferred_element_type=jnp.float32)
    up_out = jnp.dot(flat_rows, w_up[0], preferred_element_type=jnp.float32)
    hidden = (
        jax.nn.silu(gate_out) * up_out * arrived_weights.astype(jnp.float32).reshape(-1)[:, None]
    )
    hidden = hidden.astype(jnp.bfloat16).reshape(arrived_rows.shape[0], arrived_rows.shape[1], FF)
    return (attended[None], hidden.reshape(1, 1, exp_total * capacity, FF))


def solution(mesh):
    placed = (
        P("exp", "ctx", None),
        P("exp", "ctx", None),
        P("exp", "ctx", None),
        P("exp", "ctx", None),
        P(),
        P("exp", None, None),
        P("exp", None, None),
        P("exp", "ctx", None),
        P("exp", "ctx", None),
    )
    return jax.shard_map(
        per_device,
        mesh=mesh,
        in_specs=placed,
        out_specs=(P("exp", "ctx", None), P("ctx", "exp", None, None)),
        check_vma=False,
    )
```

profile of v0, /device:TPU:16, one launch (start us, length us, event | category | flops | bytes accessed | tf_op | source)
XLA Modules:
  0.0 171.3 jit_solution(7491894092021787403)
XLA Ops:
  0.6 3.7 %collective-permute-start = (bf16[128,256]{1,0:T(8,128)(2,1)}, bf16[128,256]{1,0:T(8,128)(2,1)S(1)}, u32[]{:S(2)}, u32[]{:S(2)}) collective-permute-start(bf16[128,256]{1,0:T(8,128)(2,1)} %bitcast.97), channel_id=1, source_target_pairs={{960,0},{0,64},{64,128},{128,192},{192,256},{256,320},{320,384},{3... | collective-permute-start | bytes 196616 | tf_op jit(solution)/shard_map/ppermute | solution.py:17
  4.3 0.8 copy.91
  5.1 0.1 eq.41
  5.2 0.1 reshape_squeeze.15
  5.4 0.6 reduce-window.6
  6.0 0.2 slice_reduce_fusion
  6.2 0.1 fusion.31
  6.4 0.1 select_reduce_fusion
  6.5 0.8 copy.95
  7.3 0.1 reshape_squeeze.16
  7.5 2.7 %gather_fusion.1 = bf16[384]{0:T(512)(128)(2,1)S(1)} fusion(bf16[256]{0:T(256)(128)(2,1)S(1)} %reshape_squeeze.16, s32[1024]{0:T(1024)S(1)} %pad_clamp_fusion), kind=kCustom, calls=%fused_computation.1 | custom fusion | bytes 3072 | tf_op jit(solution)/shard_map/gather | solution.py:111
  10.2 0.8 select_n.98
  11.0 15.6 %all-to-all-start.1 = ((bf16[64,1,6]{2,1,0:T(2,128)(2,1)}), bf16[64,1,6]{2,1,0:T(2,128)(2,1)S(1)}, u32[]{:S(2)}, u32[]{:S(2)}) async-start(bf16[64,1,6]{2,1,0:T(2,128)(2,1)} %select_n.98), calls=%async_computation.1 | async-start | bytes 65536 | tf_op jit(solution)/shard_map/all_to_all | solution.py:116
  26.7 0.1 broadcast_compare_fusion
  26.8 1.1 broadcast_in_dim.68
  27.9 2.8 %copy.78 = pred[2048,384]{0,1:T(8,128)(4,1)} copy(pred[2048,384]{1,0:T(8,128)(4,1)} %bitcast.89) | data formatting | bytes 1572864 | tf_op jit(solution)/shard_map/jit(_where)/broadcast_in_dim | solution.py:43
  30.6 2.1 %copy.80 = bf16[1,128,2048]{1,2,0:T(8,128)(2,1)} copy(bf16[1,128,2048]{2,1,0:T(8,128)(2,1)} %param.9) | data formatting | bytes 1048576 | tf_op args[0]
  32.7 2.8 %copy.81 = bf16[2,128,16,64]{3,2,1,0:T(8,128)(2,1)} copy(bf16[2,128,16,64]{1,3,2,0:T(8,128)(2,1)} %bitcast.91) | data formatting | bytes 1048576 | tf_op jit(solution)/shard_map/transpose | solution.py:34
  35.5 2.0 %copy.84 = bf16[1,128,2048]{1,2,0:T(8,128)(2,1)} copy(bf16[1,128,2048]{2,1,0:T(8,128)(2,1)} %param.11) | data formatting | bytes 1048576 | tf_op args[2]
  37.5 0.1 ge.20
  37.7 2.1 %collective-permute-start.1 = (bf16[128,256]{1,0:T(8,128)(2,1)S(1)}, bf16[128,256]{1,0:T(8,128)(2,1)S(1)}, u32[]{:S(2)}, u32[]{:S(2)}) collective-permute-start(bf16[128,256]{1,0:T(8,128)(2,1)S(1)} %collective-permute-done), channel_id=1, source_target_pairs={{960,0},{0,64},{64,128},{128,192},{192,256},{256,320},{320,384},{3... | collective-permute-start | bytes 196616 | tf_op jit(solution)/shard_map/ppermute | solution.py:17
  39.8 14.6 %collective-permute-done.1 = bf16[128,256]{1,0:T(8,128)(2,1)S(1)} collective-permute-done((bf16[128,256]{1,0:T(8,128)(2,1)S(1)}, bf16[128,256]{1,0:T(8,128)(2,1)S(1)}, u32[]{:S(2)}, u32[]{:S(2)}) %collective-permute-start.1) | collective-permute-done | bytes 65568 | tf_op jit(solution)/shard_map/ppermute | solution.py:17
  54.5 0.1 copy.79
  54.6 5.5 %fusion.2 = (f32[2,2048]{1,0:T(2,128)S(1)}, f32[2,384,2048]{2,1,0:T(8,128)}) fusion(pred[2048,384]{0,1:T(8,128)(4,1)} %copy.78, bf16[2,384,64]{1,2,0:T(8,128)(2,1)S(1)} %bitcast.93, bf16[2,2048,64]{2,1,0:T(8,128)(2,1)} %bitcast.88), kind=kOutput, calls=%fused_computation.6 | convolution fusion | flops 206041088 | bytes 7716864 | tf_op jit(solution)/shard_map/gqd,gsd->gqs/dot_general | solution.py:38
  60.1 0.1 reduce_max.12
  60.3 0.1 copy.85
  60.4 0.1 sub.65
  60.5 4.4 %fusion = f32[2,2048]{1,0:T(2,128)S(1)} fusion(f32[2,384,2048]{2,1,0:T(8,128)} %get-tuple-element.21, f32[2,2048]{1,0:T(2,128)S(1)} %sub.65, pred[2048,384]{0,1:T(8,128)(4,1)} %copy.78), kind=kLoop, calls=%fused_computation.4 | loop fusion | flops 6287360 | bytes 7110656 | tf_op jit(solution)/shard_map/reduce_sum | solution.py:48
  65.0 0.1 reduce_sum.39
  65.2 0.1 copy.86
  65.3 6.4 %fusion.3 = f32[2,2048,64]{2,1,0:T(8,128)} fusion(bf16[2,384,64]{1,2,0:T(8,128)(2,1)S(1)} %bitcast.94, f32[2,384,2048]{2,1,0:T(8,128)} %get-tuple-element.21, f32[2,2048]{1,0:T(2,128)S(1)} %sub.65, pred[2048,384]{0,1:T(8,128)(4,1)} %copy.78), kind=kOutput, calls=%fused_computation.7 | convolution fusion | flops 207618048 | bytes 8241152 | tf_op jit(solution)/shard_map/gqs,gsd->gqd/dot_general | solution.py:50
  71.7 3.3 %copy.89 = f32[2,128,16,64]{1,3,2,0:T(8,128)} copy(f32[2,128,16,64]{3,2,1,0:T(8,128)} %bitcast.92) | data formatting | bytes 2097152 | tf_op jit(solution)/shard_map/reshape | solution.py:51
  75.0 1.7 multiply_reduce_fusion
  76.7 0.8 copy-done.1
  77.5 1.1 bitcast_convert_fusion
  78.6 2.6 %copy.94 = f32[128,2048]{1,0:T(8,128)} copy(f32[128,2048]{0,1:T(8,128)} %bitcast_convert_fusion) | data formatting | bytes 2097152 | tf_op jit(solution)/shard_map/convert_element_type | solution.py:61
  81.2 2.2 %multiply_convert_fusion = bf16[128,2048]{1,0:T(8,128)(2,1)} fusion(f32[128,2048]{1,0:T(8,128)} %copy.94, f32[2048]{0:T(1024)S(1)} %copy-done.5, f32[128]{0:T(128)S(1)} %add_rsqrt_fusion), kind=kLoop, calls=%fused_computation.26 | loop fusion | flops 786432 | bytes 1581568 | tf_op jit(solution)/shard_map/convert_element_type | solution.py:63
  83.4 6.2 %gather_fusion = bf16[384,2048]{1,0:T(8,128)(2,1)} fusion(bf16[128,2048]{1,0:T(8,128)(2,1)} %multiply_convert_fusion, s32[1024]{0:T(1024)S(1)} %pad_clamp_fusion.1), kind=kCustom, calls=%fused_computation | custom fusion | bytes 3147264 | tf_op jit(solution)/shard_map/gather | solution.py:107
  89.6 3.7 %gather.9 = bf16[64,6,2048]{2,1,0:T(8,128)(2,1)} reshape(bf16[384,2048]{1,0:T(8,128)(2,1)} %gather_fusion) | data formatting | bytes 3145728 | tf_op jit(solution)/shard_map/gather | solution.py:107
  93.2 3.1 %broadcast_select_fusion = bf16[64,6,2048]{2,1,0:T(8,128)(2,1)} fusion(bf16[64,6,2048]{2,1,0:T(8,128)(2,1)} %gather.9, pred[64,6]{1,0:T(8,128)(4,1)S(1)} %ge.20), kind=kLoop, calls=%fused_computation.16 | loop fusion | flops 786432 | bytes 3146112 | tf_op jit(solution)/shard_map/jit(_where)/select_n | solution.py:106
  96.4 14.7 %all-to-all-start = ((bf16[64,6,2048]{2,1,0:T(8,128)(2,1)}), bf16[64,6,2048]{2,1,0:T(8,128)(2,1)}, u32[]{:S(2)}, u32[]{:S(2)}) async-start(bf16[64,6,2048]{2,1,0:T(8,128)(2,1)} %broadcast_select_fusion), calls=%async_computation | async-start | bytes 4194304 | tf_op jit(solution)/shard_map/all_to_all | solution.py:115
  111.1 0.1 convert_reduce_fusion
  111.2 0.1 reshape.299
  111.3 2.0 %copy.97 = bf16[1,128,2048]{2,1,0:T(8,128)(2,1)} copy(bf16[1,128,2048]{1,2,0:T(8,128)(2,1)} %bitcast.87) | data formatting | bytes 1048576
  113.3 49.0 %all-to-all-done = bf16[64,6,2048]{2,1,0:T(8,128)(2,1)} async-done(((bf16[64,6,2048]{2,1,0:T(8,128)(2,1)}), bf16[64,6,2048]{2,1,0:T(8,128)(2,1)}, u32[]{:S(2)}, u32[]{:S(2)}) %all-to-all-start) | async-done | bytes 1572896 | tf_op jit(solution)/shard_map/all_to_all | solution.py:115
  162.3 3.7 %reshape.297 = bf16[384,2048]{1,0:T(8,128)(2,1)} reshape(bf16[64,6,2048]{2,1,0:T(8,128)(2,1)} %all-to-all-done) | data formatting | bytes 3145728 | tf_op jit(solution)/shard_map/reshape | solution.py:118
  166.0 2.9 %fusion.7 = f32[384,768]{1,0:T(8,128)S(1)} fusion(bf16[384,2048]{1,0:T(8,128)(2,1)} %reshape.297, bf16[1,2048,768]{2,1,0:T(8,128)(2,1)S(1)} %copy-done), kind=kOutput, calls=%fused_computation.10 | convolution fusion | flops 1207959552 | bytes 5898240 | tf_op jit(solution)/shard_map/dot_general | solution.py:119
  169.0 2.3 %fusion.22 = bf16[1,1,384,768]{3,2,1,0:T(8,128)(2,1)} fusion(bf16[384,2048]{1,0:T(8,128)(2,1)S(1)} %copy-done.2, bf16[1,2048,768]{2,1,0:T(8,128)(2,1)S(1)} %copy-done.6, f32[384,768]{1,0:T(8,128)S(1)} %fusion.7, f32[384]{0:T(512)S(1)} %reshape.299), kind=kOutput, calls=%fused_computation.20 | convolution fusion | flops 1210023936 | bytes 6489600 | tf_op jit(solution)/shard_map/dot_general | solution.py:120
  (36 shorter events, 0.4 us)
Async XLA Ops:
  0.6 165.4 %copy-start = (bf16[1,2048,768]{2,1,0:T(8,128)(2,1)S(1)}, bf16[1,2048,768]{2,1,0:T(8,128)(2,1)}, u32[]{:S(2)}) copy-start(bf16[1,2048,768]{2,1,0:T(8,128)(2,1)} %param.14) | copy-start | bytes 9437188
  0.6 37.0 %collective-permute-start = (bf16[128,256]{1,0:T(8,128)(2,1)}, bf16[128,256]{1,0:T(8,128)(2,1)S(1)}, u32[]{:S(2)}, u32[]{:S(2)}) collective-permute-start(bf16[128,256]{1,0:T(8,128)(2,1)} %bitcast.97), channel_id=1, source_target_pairs={{960,0},{0,64},{64,128},{128,192},{192,256},{256,320},{320,384},{3... | collective-permute-start | bytes 196616 | tf_op jit(solution)/shard_map/ppermute | solution.py:17
  11.0 85.4 %all-to-all-start.1 = ((bf16[64,1,6]{2,1,0:T(2,128)(2,1)}), bf16[64,1,6]{2,1,0:T(2,128)(2,1)S(1)}, u32[]{:S(2)}, u32[]{:S(2)}) async-start(bf16[64,1,6]{2,1,0:T(2,128)(2,1)} %select_n.98), calls=%async_computation.1 | async-start | bytes 65536 | tf_op jit(solution)/shard_map/all_to_all | solution.py:116
  30.6 23.8 %copy-start.4 = (bf16[1,128,256]{2,1,0:T(8,128)(2,1)S(1)}, bf16[1,128,256]{2,1,0:T(8,128)(2,1)}, u32[]{:S(2)}) copy-start(bf16[1,128,256]{2,1,0:T(8,128)(2,1)} %param.10) | copy-start | bytes 196612
  37.7 16.7 %collective-permute-start.1 = (bf16[128,256]{1,0:T(8,128)(2,1)S(1)}, bf16[128,256]{1,0:T(8,128)(2,1)S(1)}, u32[]{:S(2)}, u32[]{:S(2)}) collective-permute-start(bf16[128,256]{1,0:T(8,128)(2,1)S(1)} %collective-permute-done), channel_id=1, source_target_pairs={{960,0},{0,64},{64,128},{128,192},{192,256},{256,320},{320,384},{3... | collective-permute-start | bytes 196616 | tf_op jit(solution)/shard_map/ppermute | solution.py:17
  54.6 5.7 %copy-start.3 = (f32[1,128,32]{1,2,0:T(8,128)S(1)}, f32[1,128,32]{1,2,0:T(8,128)}, u32[]{:S(2)}) copy-start(f32[1,128,32]{1,2,0:T(8,128)} %param.12) | copy-start | bytes 49156
  76.7 0.8 copy-start.1
  76.7 4.5 %copy-start.5 = (f32[2048]{0:T(1024)S(1)}, f32[2048]{0:T(1024)}, u32[]{:S(2)}) copy-start(f32[2048]{0:T(1024)} %param.13) | copy-start | bytes 24580
  96.4 65.9 %all-to-all-start = ((bf16[64,6,2048]{2,1,0:T(8,128)(2,1)}), bf16[64,6,2048]{2,1,0:T(8,128)(2,1)}, u32[]{:S(2)}, u32[]{:S(2)}) async-start(bf16[64,6,2048]{2,1,0:T(8,128)(2,1)} %broadcast_select_fusion), calls=%async_computation | async-start | bytes 4194304 | tf_op jit(solution)/shard_map/all_to_all | solution.py:115
  166.0 3.0 %copy-start.2 = (bf16[384,2048]{1,0:T(8,128)(2,1)S(1)}, bf16[384,2048]{1,0:T(8,128)(2,1)}, u32[]{:S(2)}) copy-start(bf16[384,2048]{1,0:T(8,128)(2,1)} %reshape.297) | copy-start | bytes 4718596
  166.0 3.0 %copy-start.6 = (bf16[1,2048,768]{2,1,0:T(8,128)(2,1)S(1)}, bf16[1,2048,768]{2,1,0:T(8,128)(2,1)}, u32[]{:S(2)}) copy-start(bf16[1,2048,768]{2,1,0:T(8,128)(2,1)} %param.15) | copy-start | bytes 9437188
where the time goes:
time: 172 us; the launch traced here: 171 us
  waiting for transfers between devices  63.6 us (37%)
  local copies, waits for them, and re-layouts  39.8 us (23%)
  starting transfers between devices  36 us (21%)
  matrix products  17.2 us (10%)
  other arithmetic  13.8 us (8%)
    all_to_all x1, waiting for transfers between devices, per_device(): lax.all_to_all(payload, 'exp', split_axis=0, concat_axis=0, tiled=True)  49 us
    all_to_all x1, starting transfers between devices, per_device(): lax.all_to_all(slot_weights, 'exp', split_axis=0, concat_axis=0, tiled=True)  15.6 us
    all_to_all x1, starting transfers between devices, per_device(): lax.all_to_all(payload, 'exp', split_axis=0, concat_axis=0, tiled=True)  14.7 us
    ppermute x2, waiting for transfers between devices, passed_along(): return lax.ppermute(block, axis, route)  14.6 us
    gather x2, local copies, waits for them, and re-layouts, per_device(): outgoing[clamped // IN_FLIGHT]  9.86 us
    unnamed x19, local copies, waits for them, and re-layouts  8.54 us
    dot_general x1, matrix products, attend_local(): jnp.einsum('gqs,gsd->gqd', powers_low, value_rows, preferred_element_type...  6.44 us
    ppermute x2, starting transfers between devices, passed_along(): return lax.ppermute(block, axis, route)  5.77 us
  transfers between devices with their start and end apart: 4, of which 2 were waited for; matrix products, arithmetic and copies ran while one was open for 36% of the time, Pallas kernels for 0%

commit v1 on v0

v1 whole, which is shorter than its diff:
```python
import functools

import jax
import jax.numpy as jnp
from jax import lax
from jax.experimental import pallas as pl
from jax.experimental.pallas import tpu as pltpu
from jax.sharding import PartitionSpec as P

HQ = 32
KVH = 2
HD = 64
FF = 768
D = HQ * HD
TOK = 128
HALF = TOK // 2
EXPERTS = 64
CAP = 6
LANES = 128
MSG_ROWS = 8
MAIN = CAP * D // MSG_ROWS
TAIL = D - MAIN
PAYLOAD = MAIN + LANES
LAST_LANES = (((1,), (1,)), ((), ()))
PAIRS = KVH * 8
QUADS = PAIRS // 2


def iota(shape, dim):
    return lax.broadcasted_iota(jnp.int32, shape, dim)


def as_bf16(mask):
    return jnp.where(mask, 1.0, 0.0).astype(jnp.bfloat16)


def dot_f32(a, b):
    return jnp.dot(a, b, preferred_element_type=jnp.float32)


def dot_t(a, b):
    return lax.dot_general(a, b, LAST_LANES, preferred_element_type=jnp.float32)


def attend_kernel(
    q_ref, kv0_ref, kv1_ref, kv2_ref, prior_ref, lse_ref, gain_ref, ids_ref, rw_ref,
    out_ref, send_ref, kb_ref, vb_ref, lse0_ref, lse1_ref, sq_ref,
):
    block = lax.axis_index("ctx")
    kv_refs = (kv0_ref, kv1_ref, kv2_ref)
    eye = as_bf16(iota((LANES, LANES), 0) == iota((LANES, LANES), 1))
    low = iota((1, LANES), 1) < HALF
    for group in range(KVH):
        first = lse_ref[group * 16 : group * 16 + 8, :]
        second = lse_ref[group * 16 + 8 : group * 16 + 16, :]
        rows = slice(group * 8, group * 8 + 8)
        lse0_ref[rows, :] = jnp.where(low, first, pltpu.roll(second, HALF, 1))
        lse1_ref[rows, :] = jnp.where(low, pltpu.roll(first, HALF, 1), second)
    sq_ref[...] = jnp.zeros_like(sq_ref)

    def spread(piece_ref, half, column, scale):
        piece = piece_ref[half * HALF : (half + 1) * HALF, column : column + LANES]
        piece = piece.astype(jnp.float32) * scale
        turned = pltpu.roll(piece, HALF, 1)
        zero = jnp.zeros_like(piece)
        return (
            (jnp.where(low, piece, zero), jnp.where(low, zero, turned)),
            (jnp.where(low, turned, zero), jnp.where(low, zero, piece)),
        )

    def lay(pieces, start):
        count = len(pieces) * HALF
        for place, (which, half) in enumerate(pieces):
            keys = spread(kv_refs[which], half, 0, HD ** -0.5)
            values = spread(kv_refs[which], half, LANES, 1.0)
            for group in range(KVH):
                for parity in range(2):
                    row = start + parity * count + place * HALF
                    kb_ref[group, row : row + HALF, :] = keys[group][parity].astype(jnp.bfloat16)
                    vb_ref[group, row : row + HALF, :] = values[group][parity].astype(jnp.bfloat16)

    def half_of(quad, group, half, pieces, start, lse_half_ref):
        rows = slice(half * HALF, (half + 1) * HALF)
        pair = group * 8 + lax.rem(quad, 4)
        columns = [pl.ds(pl.multiple_of((pair + 4 * i) * LANES, LANES), LANES) for i in range(2)]
        queries = jnp.concatenate([q_ref[rows, c] for c in columns], axis=0)
        prior = jnp.concatenate([prior_ref[rows, c] for c in columns], axis=0)
        count = len(pieces) * HALF
        keys = kb_ref[group, start : start + 2 * count, :]
        values = vb_ref[group, start : start + 2 * count, :]
        scores = dot_t(keys, queries)
        prior_t = dot_t(eye, prior)
        powers, shares = [], []
        for parity in range(2):
            parts = []
            for place, (_, _, rule) in enumerate(pieces):
                row = parity * count + place * HALF
                part = scores[row : row + HALF, :]
                if rule == "tri":
                    ahead = iota((HALF, LANES), 0) > (iota((HALF, LANES), 1) & (HALF - 1))
                    part = jnp.where(ahead, -1e30, part)
                elif rule is not None:
                    part = jnp.where(block == rule, -1e30, part)
                parts.append(part)
            own = jnp.concatenate(parts, axis=0)
            logs = lse_half_ref[pl.ds(group * 8 + 2 * lax.rem(quad, 4) + parity, 1), :]
            top = jnp.maximum(jnp.max(own, axis=0, keepdims=True), logs)
            power = jnp.exp(own - top)
            carried = jnp.exp(logs - top)
            total = carried + jnp.sum(power, axis=0, keepdims=True)
            powers.append(power.astype(jnp.bfloat16))
            shares.append((carried, 1.0 / total))
        mixed = lax.dot_general(
            values, jnp.concatenate(powers, axis=0), (((0,), (0,)), ((), ())),
            preferred_element_type=jnp.float32,
        )
        result = jnp.concatenate(
            [
                (carried * prior_t[p * HALF : (p + 1) * HALF] + mixed[p * HALF : (p + 1) * HALF])
                * inverse
                for p, (carried, inverse) in enumerate(shares)
            ],
            axis=0,
        ).astype(jnp.bfloat16)
        upright = dot_t(eye, result)
        sq_ref[rows, :] += upright[:HALF] * upright[:HALF] + upright[HALF:] * upright[HALF:]
        for i, c in enumerate(columns):
            out_ref[rows, c] = upright[i * HALF : (i + 1) * HALF].astype(jnp.bfloat16)

    def attend(first_half, second_half):
        begin = 2 * HALF * len(first_half)
        lay([piece[:2] for piece in first_half], 0)
        lay([piece[:2] for piece in second_half], begin)

        @pl.loop(0, QUADS)
        def _(quad):
            group = lax.div(quad, 4)
            half_of(quad, group, 0, first_half, 0, lse0_ref)
            half_of(quad, group, 1, second_half, begin, lse1_ref)

    @pl.when(block >= 2)
    def _():
        attend(
            [(0, 0, "tri"), (1, 0, None), (2, 0, None)],
            [(0, 0, None), (0, 1, "tri"), (1, 0, None), (2, 0, None)],
        )

    @pl.when(block < 2)
    def _():
        attend(
            [(0, 0, "tri"), (1, 0, 0)],
            [(0, 0, None), (0, 1, "tri"), (1, 0, None), (1, 1, 1), (2, 0, None), (2, 1, None)],
        )

    mean = jnp.sum(sq_ref[...], axis=-1, keepdims=True) * (1.0 / D)
    inverse = lax.rsqrt(mean + 1e-06)
    normed = (out_ref[...].astype(jnp.float32) * inverse * gain_ref[...]).astype(jnp.bfloat16)

    experts = iota((EXPERTS, TOK), 0)
    chosen = [ids_ref[j : j + 1, :] == experts for j in range(2)]
    named = chosen[0] | chosen[1]
    before = as_bf16(iota((TOK, TOK), 0) < iota((TOK, TOK), 1))
    rank = dot_f32(as_bf16(named), before)
    code = jnp.where(named, rank, -1.0).astype(jnp.bfloat16)
    weights = rw_ref[...].astype(jnp.float32)
    weight = (
        jnp.where(chosen[0], weights[0:1, :], 0.0) + jnp.where(chosen[1], weights[1:2, :], 0.0)
    ).astype(jnp.bfloat16)
    total_rows = EXPERTS * MSG_ROWS
    repeat = as_bf16(iota((total_rows, EXPERTS), 0) // MSG_ROWS == iota((total_rows, EXPERTS), 1))
    codes = dot_f32(repeat, code).astype(jnp.int32)
    place = iota((total_rows, TOK), 0) & (MSG_ROWS - 1)
    picked = codes == place
    main = as_bf16(picked)
    spread_weights = jnp.where(picked, dot_f32(repeat, weight), 0.0).astype(jnp.bfloat16)
    send_ref[:, MAIN:] = dot_f32(
        spread_weights, jnp.ones((TOK, LANES), jnp.bfloat16)
    ).astype(jnp.bfloat16)
    last = normed[:, MAIN:]
    for k in range(3):
        wanted = jnp.where(place == 6, k, jnp.where(place == 7, 3 + k, -2))
        select = jnp.concatenate([main, as_bf16(codes == wanted)], axis=1)
        columns = slice(k * TAIL, (k + 1) * TAIL)
        rows = jnp.concatenate([normed[:, columns], last], axis=0)
        send_ref[:, columns] = dot_f32(select, rows).astype(jnp.bfloat16)


def attend_and_pack(query, blocks, prior, logs, gain, ids, weights):
    vmem = pl.BlockSpec(memory_space=pltpu.VMEM)
    return pl.pallas_call(
        attend_kernel,
        out_shape=(
            jax.ShapeDtypeStruct((TOK, D), jnp.bfloat16),
            jax.ShapeDtypeStruct((EXPERTS * MSG_ROWS, PAYLOAD), jnp.bfloat16),
        ),
        in_specs=[vmem] * 9,
        out_specs=(vmem, vmem),
        scratch_shapes=[
            pltpu.VMEM((KVH, 16 * HALF, LANES), jnp.bfloat16),
            pltpu.VMEM((KVH, 16 * HALF, LANES), jnp.bfloat16),
            pltpu.VMEM((16, LANES), jnp.float32),
            pltpu.VMEM((16, LANES), jnp.float32),
            pltpu.VMEM((TOK, LANES), jnp.float32),
        ],
        cost_estimate=pl.CostEstimate(
            flops=2_000_000_000, bytes_accessed=4_000_000, transcendentals=1_000_000
        ),
        name="attend_and_pack",
    )(query, *blocks, prior, logs, gain, ids, weights)


def expert_kernel(got_ref, gate_ref, up_ref, out_ref, rows_ref, weight_ref):
    step_rows, step_slots = 16 * MSG_ROWS, 16 * CAP
    slot, source = iota((step_slots, step_rows), 0), iota((step_slots, step_rows), 1)
    rank, sender = lax.rem(slot, CAP), lax.div(slot, CAP) * MSG_ROWS
    main = as_bf16(source == sender + rank)
    tails = [
        as_bf16(
            ((rank == k) & (source == sender + 6)) | ((rank == 3 + k) & (source == sender + 7))
        )
        for k in range(3)
    ]
    tail = jnp.concatenate(tails, axis=1)
    for step in range(EXPERTS // 16):
        rows = slice(step * step_rows, (step + 1) * step_rows)
        slots = slice(step * step_slots, (step + 1) * step_slots)
        rows_ref[slots, :MAIN] = dot_f32(main, got_ref[rows, :MAIN]).astype(jnp.bfloat16)
        stacked = jnp.concatenate(
            [got_ref[rows, k * TAIL : (k + 1) * TAIL] for k in range(3)], axis=0
        )
        rows_ref[slots, MAIN:] = dot_f32(tail, stacked).astype(jnp.bfloat16)
        weight_ref[slots, :] = dot_f32(main, got_ref[rows, MAIN:])

    width = 256

    @pl.loop(0, FF // width)
    def _(tile):
        columns = pl.ds(pl.multiple_of(tile * width, width), width)
        gate = dot_f32(rows_ref[...], gate_ref[:, columns])
        up = dot_f32(rows_ref[...], up_ref[:, columns])
        weight = weight_ref[...]
        weight = jnp.concatenate([weight] * (width // LANES), axis=1)
        out_ref[:, columns] = (jax.nn.silu(gate) * up * weight).astype(jnp.bfloat16)


def expert_rows(got, w_gate, w_up):
    vmem = pl.BlockSpec(memory_space=pltpu.VMEM)
    return pl.pallas_call(
        expert_kernel,
        out_shape=jax.ShapeDtypeStruct((EXPERTS * CAP, FF), jnp.bfloat16),
        in_specs=[vmem] * 3,
        out_specs=vmem,
        scratch_shapes=[
            pltpu.VMEM((EXPERTS * CAP, D), jnp.bfloat16),
            pltpu.VMEM((EXPERTS * CAP, LANES), jnp.float32),
        ],
        cost_estimate=pl.CostEstimate(
            flops=2_600_000_000, bytes_accessed=9_000_000, transcendentals=300_000
        ),
        name="expert_rows",
    )(got, w_gate, w_up)


def passed_along(block, distance):
    count = lax.axis_size("ctx")
    route = [((i - distance) % count, i) for i in range(count)]
    return lax.ppermute(block, "ctx", route)


def per_device(
    query, key_value, prior_out, prior_lse, norm_gain, w_gate, w_up, expert_ids, route_weight
):
    own = key_value[0]
    blocks = (own, passed_along(own, 1), passed_along(own, 2))
    attended, payload = attend_and_pack(
        query[0], blocks, prior_out[0], prior_lse[0].T, norm_gain[None, :],
        expert_ids[0].T, route_weight[0].T,
    )
    got = lax.all_to_all(
        payload.reshape(EXPERTS, MSG_ROWS, PAYLOAD), "exp", split_axis=0, concat_axis=0, tiled=True
    )
    hidden = expert_rows(got.reshape(EXPERTS * MSG_ROWS, PAYLOAD), w_gate[0], w_up[0])
    return attended[None], hidden[None, None]


def solution(mesh):
    placed = (
        P("exp", "ctx", None),
        P("exp", "ctx", None),
        P("exp", "ctx", None),
        P("exp", "ctx", None),
        P(),
        P("exp", None, None),
        P("exp", None, None),
        P("exp", "ctx", None),
        P("exp", "ctx", None),
    )
    return jax.shard_map(
        per_device,
        mesh=mesh,
        in_specs=placed,
        out_specs=(P("exp", "ctx", None), P("ctx", "exp", None, None)),
        check_vma=False,
    )
```

time: 172 us -> 107 us (0.62)
  blocking collectives: 0 us -> 61.4 us
  waiting for transfers between devices: 63.6 us -> 17.4 us
  local copies, waits for them, and re-layouts: 39.8 us -> 0.63 us
  starting transfers between devices: 36 us -> 7.43 us
  Pallas kernels: 0 us -> 18.7 us
  matrix products: 17.2 us -> 0 us
  other arithmetic: 13.8 us -> 0 us
    all_to_all x0 -> x1, blocking collectives: none -> 61.4 us  [per_device(): lax.all_to_all(payload.reshape(EXPERTS, MSG_ROWS, PAYLOAD), 'exp', split_...]
    all_to_all x2 -> x0, waiting for transfers between devices: 49 us -> none  [the longest x1 49 us: per_device(): lax.all_to_all(payload, 'exp', split_axis=0, concat_axis=0, tiled=True)]
    all_to_all x2 -> x0, starting transfers between devices: 30.2 us -> none  [the longest x1 15.6 us: per_device(): lax.all_to_all(slot_weights, 'exp', split_axis=0, concat_axis=0, tiled=True)]
    pallas_call x0 -> x2, Pallas kernels: none -> 18.7 us  [the longest x1 10.8 us: attend_and_pack(): pl.pallas_call(attend_kernel, out_shape=(jax.ShapeDtypeStruct((TOK, D), j...]
    dot_general x4 -> x0, matrix products: 17.2 us -> none  [the longest x1 6.44 us: attend_local(): jnp.einsum('gqs,gsd->gqd', powers_low, value_rows, preferred_element_type...]
    gather x3 -> x0, local copies, waits for them, and re-layouts: 12.6 us -> none  [the longest x2 9.86 us: per_device(): outgoing[clamped // IN_FLIGHT]]
    unnamed x19 -> x4, local copies, waits for them, and re-layouts: 8.54 us -> 0.63 us
    reshape x2 -> x0, local copies, waits for them, and re-layouts: 7.01 us -> none  [the longest x1 3.7 us: per_device(): flat_rows = arrived_rows.reshape(-1, arrived_rows.shape[-1])]
  transfers between devices with their start and end apart: 4 -> 2, of which waited for: 2 -> 2; matrix products, arithmetic and copies ran while one was open for 36% -> 0% of each run, Pallas kernels for 0% -> 0%
where the time goes in v1:
time: 107 us; the launch traced here: 106 us
  blocking collectives  61.4 us (57%)
  Pallas kernels  18.7 us (17%)
  waiting for transfers between devices  17.4 us (16%)
  starting transfers between devices  7.43 us (7%)
    all_to_all x1, blocking collectives, per_device(): lax.all_to_all(payload.reshape(EXPERTS, MSG_ROWS, PAYLOAD), 'exp', split_...  61.4 us
    ppermute x2, waiting for transfers between devices, passed_along(): return lax.ppermute(block, 'ctx', route)  17.4 us
    pallas_call x1, Pallas kernels, attend_and_pack(): pl.pallas_call(attend_kernel, out_shape=(jax.ShapeDtypeStruct((TOK, D), j...  10.8 us
    pallas_call x1, Pallas kernels, expert_rows(): pl.pallas_call(expert_kernel, out_shape=jax.ShapeDtypeStruct((EXPERTS * C...  7.93 us
    ppermute x2, starting transfers between devices, passed_along(): return lax.ppermute(block, 'ctx', route)  7.43 us
  transfers between devices with their start and end apart: 2, of which 2 were waited for; matrix products, arithmetic and copies ran while one was open for 0% of the time, Pallas kernels for 0%

profile of v1, /device:TPU:16, one launch (start us, length us, event | category | flops | bytes accessed | tf_op | source)
XLA Modules:
  0.0 106.3 jit_solution(7714902782651762151)
XLA Ops:
  0.6 4.9 %collective-permute-start.1 = (bf16[128,256]{1,0:T(8,128)(2,1)}, bf16[128,256]{1,0:T(8,128)(2,1)S(1)}, u32[]{:S(2)}, u32[]{:S(2)}) collective-permute-start(bf16[128,256]{1,0:T(8,128)(2,1)} %bitcast.25), channel_id=1, source_target_pairs={{896,0},{960,64},{0,128},{64,192},{128,256},{192,320},{256,384},{3... | collective-permute-start | bytes 196616 | tf_op jit(solution)/shard_map/ppermute | solution.py:267
  5.6 2.5 %collective-permute-start = (bf16[128,256]{1,0:T(8,128)(2,1)}, bf16[128,256]{1,0:T(8,128)(2,1)S(1)}, u32[]{:S(2)}, u32[]{:S(2)}) collective-permute-start(bf16[128,256]{1,0:T(8,128)(2,1)} %bitcast.26), channel_id=1, source_target_pairs={{960,0},{0,64},{64,128},{128,192},{192,256},{256,320},{320,384},{3... | collective-permute-start | bytes 196616 | tf_op jit(solution)/shard_map/ppermute | solution.py:267
  8.1 15.8 %collective-permute-done.1.kv2_ref = bf16[128,256]{1,0:T(8,128)(2,1)S(1)} collective-permute-done((bf16[128,256]{1,0:T(8,128)(2,1)}, bf16[128,256]{1,0:T(8,128)(2,1)S(1)}, u32[]{:S(2)}, u32[]{:S(2)}) %collective-permute-start.1) | collective-permute-done | bytes 65568 | tf_op jit(solution)/shard_map/ppermute | solution.py:267
  23.9 0.0 copy-start
  23.9 1.6 %collective-permute-done.kv1_ref = bf16[128,256]{1,0:T(8,128)(2,1)S(1)} collective-permute-done((bf16[128,256]{1,0:T(8,128)(2,1)}, bf16[128,256]{1,0:T(8,128)(2,1)S(1)}, u32[]{:S(2)}, u32[]{:S(2)}) %collective-permute-start) | collective-permute-done | bytes 65568 | tf_op jit(solution)/shard_map/ppermute | solution.py:267
  25.5 0.0 copy-start.1
  25.5 0.0 copy-done
  25.5 0.6 copy-done.1
  26.1 10.8 %attend_and_pack.1 = (bf16[128,2048]{1,0:T(8,128)(2,1)}, bf16[512,1664]{1,0:T(8,128)(2,1)}) custom-call(bf16[128,2048]{1,0:T(8,128)(2,1)} %bitcast.23, bf16[128,256]{1,0:T(8,128)(2,1)} %bitcast.27, bf16[128,256]{1,0:T(8,128)(2,1)} %copy-done.1, bf16[128,256]{1,0:T(8,128)(2,1)} %copy-done, bf16[128,2048]{1,0:T(8,128)(2,1)} %bitcast.24, f32[32,128]{1,0:T(8,128)} %bitcast.28, ...), custom_call_target="tpu_custom_call" | custom-call | flops 2000000000 | bytes 4000000 | tf_op jit(solution)/shard_map/attend_and_pack/pallas_call | solution.py:190
  36.9 61.4 %all_to_all.5 = bf16[64,8,1664]{2,1,0:T(8,128)(2,1)} all-to-all(bf16[64,8,1664]{2,1,0:T(8,128)(2,1)} %bitcast.19), channel_id=1, replica_groups=mesh['ctx'=16,'exp'=64] {'exp'}, dimensions={0} | all-to-all | bytes 3407872 | tf_op jit(solution)/shard_map/all_to_all | solution.py:279
  98.3 7.9 %expert_rows.1 = bf16[384,768]{1,0:T(8,128)(2,1)} custom-call(bf16[512,1664]{1,0:T(8,128)(2,1)} %bitcast.20, bf16[2048,768]{1,0:T(8,128)(2,1)} %bitcast.21, bf16[2048,768]{1,0:T(8,128)(2,1)} %bitcast.22), custom_call_target="tpu_custom_call" | custom-call | flops 2600000000 | bytes 9000000 | tf_op jit(solution)/shard_map/expert_rows/pallas_call | solution.py:248
Async XLA Ops:
  0.6 23.3 %collective-permute-start.1 = (bf16[128,256]{1,0:T(8,128)(2,1)}, bf16[128,256]{1,0:T(8,128)(2,1)S(1)}, u32[]{:S(2)}, u32[]{:S(2)}) collective-permute-start(bf16[128,256]{1,0:T(8,128)(2,1)} %bitcast.25), channel_id=1, source_target_pairs={{896,0},{960,64},{0,128},{64,192},{128,256},{192,320},{256,384},{3... | collective-permute-start | bytes 196616 | tf_op jit(solution)/shard_map/ppermute | solution.py:267
  5.6 19.9 %collective-permute-start = (bf16[128,256]{1,0:T(8,128)(2,1)}, bf16[128,256]{1,0:T(8,128)(2,1)S(1)}, u32[]{:S(2)}, u32[]{:S(2)}) collective-permute-start(bf16[128,256]{1,0:T(8,128)(2,1)} %bitcast.26), channel_id=1, source_target_pairs={{960,0},{0,64},{64,128},{128,192},{192,256},{256,320},{320,384},{3... | collective-permute-start | bytes 196616 | tf_op jit(solution)/shard_map/ppermute | solution.py:267
  23.9 1.6 %copy-start = (bf16[128,256]{1,0:T(8,128)(2,1)}, bf16[128,256]{1,0:T(8,128)(2,1)S(1)}, u32[]{:S(2)}) copy-start(bf16[128,256]{1,0:T(8,128)(2,1)S(1)} %collective-permute-done.1.kv2_ref) | copy-start | bytes 196612
  25.5 0.6 copy-start.1

commit v2 on v1

v2 whole, which is shorter than its diff:
```python
import jax
import jax.numpy as jnp
from jax import lax
from jax.experimental import pallas as pl
from jax.experimental.pallas import tpu as pltpu
from jax.sharding import PartitionSpec as P

HQ = 32
KVH = 2
HD = 64
FF = 768
D = HQ * HD
TOK = 128
HALF = TOK // 2
EXPERTS = 64
CAP = 6
LANES = 128
MSG_ROWS = 8
MAIN = CAP * D // MSG_ROWS
TAIL = D - MAIN
PAYLOAD = MAIN + LANES
LAST_LANES = (((1,), (1,)), ((), ()))
PAIRS = KVH * 8
QUADS = PAIRS // 2


def iota(shape, dim):
    return lax.broadcasted_iota(jnp.int32, shape, dim)


def as_bf16(mask):
    return jnp.where(mask, 1.0, 0.0).astype(jnp.bfloat16)


def dot_f32(a, b):
    return jnp.dot(a, b, preferred_element_type=jnp.float32)


def dot_t(a, b):
    return lax.dot_general(a, b, LAST_LANES, preferred_element_type=jnp.float32)


def spread(piece, scale):
    low = iota((1, LANES), 1) < HD
    piece = piece.astype(jnp.float32) * scale
    turned = pltpu.roll(piece, HD, 1)
    zero = jnp.zeros_like(piece)
    blocks = (
        (jnp.where(low, piece, zero), jnp.where(low, zero, turned)),
        (jnp.where(low, turned, zero), jnp.where(low, zero, piece)),
    )
    return [[block.astype(jnp.bfloat16) for block in pair] for pair in blocks]


def lay(pieces):
    keys = [spread(piece[:, :LANES], HD ** -0.5) for piece in pieces]
    values = [spread(piece[:, LANES:], 1.0) for piece in pieces]

    def stack(blocks, group):
        return jnp.concatenate(
            [block[group][parity] for parity in range(2) for block in blocks], axis=0
        )

    eye = unit()
    return (
        [stack(keys, group) for group in range(KVH)],
        [dot_t(eye, stack(values, group)).astype(jnp.bfloat16) for group in range(KVH)],
    )


def unit():
    return as_bf16(iota((LANES, LANES), 0) == iota((LANES, LANES), 1))


def ahead():
    return iota((HALF, LANES), 0) > (iota((HALF, LANES), 1) & (HALF - 1))


def pairs_of(quad):
    pair = quad // 4 * 8 + quad % 4
    return pair, pair + 4


def both(rows):
    return jnp.concatenate([jnp.broadcast_to(row, (HD, row.shape[1])) for row in rows], axis=0)


def slots(ids, weights, pick_ref, weight_ref):
    experts = iota((EXPERTS, TOK), 0)
    chosen = [ids[j : j + 1, :] == experts for j in range(2)]
    named = chosen[0] | chosen[1]
    before = as_bf16(iota((TOK, TOK), 0) < iota((TOK, TOK), 1))
    rank = dot_f32(as_bf16(named), before)
    code = jnp.where(named, rank, -1.0).astype(jnp.bfloat16)
    weights = weights.astype(jnp.float32)
    weight = (
        jnp.where(chosen[0], weights[0:1, :], 0.0) + jnp.where(chosen[1], weights[1:2, :], 0.0)
    ).astype(jnp.bfloat16)
    both_codes = jnp.concatenate([code, weight], axis=1)
    step = 128
    ones = jnp.ones((TOK, LANES), jnp.bfloat16)
    place = iota((step, TOK), 0) & (MSG_ROWS - 1)
    for start in range(0, EXPERTS * MSG_ROWS, step):
        rows = slice(start, start + step)
        repeat = as_bf16(
            (iota((step, EXPERTS), 0) + start) // MSG_ROWS == iota((step, EXPERTS), 1)
        )
        repeated = dot_f32(repeat, both_codes)
        codes = repeated[:, :TOK].astype(jnp.int32)
        picked = codes == place
        pick_ref[rows, :TOK] = as_bf16(picked)
        carried = jnp.where(picked, repeated[:, TOK:], 0.0).astype(jnp.bfloat16)
        weight_ref[rows, :] = dot_f32(carried, ones).astype(jnp.bfloat16)
        for k in range(3):
            wanted = jnp.where(place == 6, k, jnp.where(place == 7, 3 + k, -2))
            pick_ref[rows, (k + 1) * TOK : (k + 2) * TOK] = as_bf16(codes == wanted)


def front_kernel(
    q_hbm, kv_hbm, prior_hbm, lse_hbm, ids_hbm, rw_hbm,
    qs_ref, mix_ref, top_ref, sum_ref, pick_ref, weight_ref,
    kv_ref, prior_ref, lse_ref, ids_ref, rw_ref, sems,
):
    copies = [
        pltpu.make_async_copy(kv_hbm, kv_ref, sems.at[0]),
        pltpu.make_async_copy(lse_hbm, lse_ref, sems.at[1]),
        pltpu.make_async_copy(ids_hbm, ids_ref, sems.at[2]),
        pltpu.make_async_copy(rw_hbm, rw_ref, sems.at[3]),
    ]
    for copy in copies:
        copy.start()
    moves = []
    for quad in range(QUADS):
        for half in range(2):
            for i, pair in enumerate(pairs_of(quad)):
                rows, columns = slice(half * HALF, (half + 1) * HALF), slice(pair * LANES, (pair + 1) * LANES)
                target = slice(half * LANES + i * HALF, half * LANES + (i + 1) * HALF)
                moves.append(
                    pltpu.make_async_copy(q_hbm.at[rows, columns], qs_ref.at[quad, target, :], sems.at[4])
                )
                moves.append(
                    pltpu.make_async_copy(prior_hbm.at[rows, columns], prior_ref.at[quad, target, :], sems.at[5])
                )
    for move in moves:
        move.start()
    for copy in copies:
        copy.wait()
    slots(ids_ref[...], rw_ref[...], pick_ref, weight_ref)
    keys, values = lay([kv_ref[:HALF, :], kv_ref[HALF:, :]])
    eye = unit()
    low = iota((1, LANES), 1) < HALF
    late = ahead()
    for move in moves:
        move.wait()

    def scores(quad):
        group = quad // 4
        early = jnp.concatenate([keys[group][:HALF], keys[group][2 * HALF : 3 * HALF]], axis=0)
        return (
            dot_t(early, qs_ref[quad, :LANES, :]),
            dot_t(keys[group], qs_ref[quad, LANES:, :]),
        )

    def soften(quad, found):
        group, head = quad // 4, quad // 4 * 16 + 2 * (quad % 4)
        for half in range(2):
            powers, carries = [], []
            for parity in range(2):
                first = lse_ref[head + parity : head + parity + 1, :]
                second = lse_ref[head + parity + 8 : head + parity + 9, :]
                if half == 0:
                    logs = jnp.where(low, first, pltpu.roll(second, HALF, 1))
                    own = found[0][parity * HALF : (parity + 1) * HALF]
                    own = jnp.where(late, -1e30, own)
                else:
                    logs = jnp.where(low, pltpu.roll(first, HALF, 1), second)
                    own = found[1][parity * TOK : (parity + 1) * TOK]
                    own = jnp.concatenate(
                        [own[:HALF], jnp.where(late, -1e30, own[HALF:])], axis=0
                    )
                top = jnp.maximum(jnp.max(own, axis=0, keepdims=True), logs)
                power = jnp.exp(own - top)
                carried = jnp.exp(logs - top)
                row = quad * 4 + half * 2 + parity
                top_ref[row : row + 1, :] = top
                sum_ref[row : row + 1, :] = carried + jnp.sum(power, axis=0, keepdims=True)
                powers.append(power.astype(jnp.bfloat16))
                carries.append(carried)
            turned = values[group]
            if half == 0:
                turned = jnp.concatenate([turned[:, :HALF], turned[:, 2 * HALF : 3 * HALF]], axis=1)
            mixed = dot_f32(turned, jnp.concatenate(powers, axis=0))
            prior = dot_t(eye, prior_ref[quad, half * LANES : (half + 1) * LANES, :])
            mix_ref[quad, :, half * LANES : (half + 1) * LANES] = both(carries) * prior + mixed

    held = scores(0)
    for quad in range(QUADS):
        following = scores(quad + 1) if quad + 1 < QUADS else None
        soften(quad, held)
        held = following


def back_kernel(
    kv1_ref, kv2_ref, qs_ref, mix_ref, top_ref, sum_ref, pick_ref, weight_ref, gain_ref,
    out_ref, send_ref,
):
    block = lax.axis_index("ctx")
    eye = unit()

    def scores_of(keys, quad, tokens):
        return dot_t(keys[quad // 4], qs_ref[quad, tokens, :])

    def soften(quad, found, count, values, tokens, masks):
        powers, scales, inverses = [], [], []
        for parity in range(2):
            new = found[parity * count : (parity + 1) * count]
            if masks:
                new = jnp.concatenate(
                    [
                        part if rule is None else jnp.where(block == rule, -1e30, part)
                        for part, rule in (
                            (new[i * HALF : (i + 1) * HALF], rule) for i, rule in enumerate(masks)
                        )
                    ],
                    axis=0,
                )
            halves = range(tokens.start // LANES, tokens.stop // LANES)
            rows = [quad * 4 + half * 2 + parity for half in halves]
            old = jnp.concatenate([top_ref[row : row + 1, :] for row in rows], axis=1)
            total = jnp.concatenate([sum_ref[row : row + 1, :] for row in rows], axis=1)
            top = jnp.maximum(jnp.max(new, axis=0, keepdims=True), old)
            scale = jnp.exp(old - top)
            power = jnp.exp(new - top)
            total = total * scale + jnp.sum(power, axis=0, keepdims=True)
            powers.append(power.astype(jnp.bfloat16))
            inverse = 1.0 / total
            scales.append(scale * inverse)
            inverses.append(inverse)
        mixed = dot_f32(values[quad // 4], jnp.concatenate(powers, axis=0))
        result = mix_ref[quad, :, tokens] * both(scales) + mixed * both(inverses)
        return result.astype(jnp.bfloat16)

    def finish(quad, result, tokens):
        for place, half in enumerate(range(tokens.start // LANES, tokens.stop // LANES)):
            upright = dot_t(eye, result[:, place * LANES : (place + 1) * LANES])
            for i, pair in enumerate(pairs_of(quad)):
                out_ref[half * HALF : (half + 1) * HALF, pair * LANES : (pair + 1) * LANES] = (
                    upright[i * HALF : (i + 1) * HALF].astype(jnp.bfloat16)
                )

    def run(tasks):
        found, results = {}, {}
        for step in range(len(tasks) + 2):
            if step < len(tasks):
                quad, keys, _, _, tokens, _ = tasks[step]
                found[step] = scores_of(keys, quad, tokens)
            if 1 <= step <= len(tasks):
                quad, _, values, count, tokens, masks = tasks[step - 1]
                results[step - 1] = soften(quad, found.pop(step - 1), count, values, tokens, masks)
            if step >= 2:
                quad, tokens = tasks[step - 2][0], tasks[step - 2][4]
                finish(quad, results.pop(step - 2), tokens)

    @pl.when(block >= 2)
    def _():
        keys, values = lay([kv1_ref[:HALF, :], kv2_ref[:HALF, :]])
        everyone = slice(0, 2 * LANES)
        run([(quad, keys, values, TOK, everyone, None) for quad in range(QUADS)])

    @pl.when(block < 2)
    def _():
        near_keys, near_values = lay([kv1_ref[:HALF, :]])
        all_keys, all_values = lay(
            [kv1_ref[:HALF, :], kv1_ref[HALF:, :], kv2_ref[:HALF, :], kv2_ref[HALF:, :]]
        )
        tasks = []
        for quad in range(QUADS):
            tasks.append((quad, near_keys, near_values, HALF, slice(0, LANES), [0]))
            tasks.append(
                (quad, all_keys, all_values, 4 * HALF, slice(LANES, 2 * LANES), [None, 1, None, None])
            )
        run(tasks)

    squares = jnp.zeros((TOK, LANES), jnp.float32)
    for pair in range(PAIRS):
        value = out_ref[:, pair * LANES : (pair + 1) * LANES].astype(jnp.float32)
        squares += value * value
    inverse = lax.rsqrt(jnp.sum(squares, axis=-1, keepdims=True) * (1.0 / D) + 1e-06)

    def normed(columns):
        value = out_ref[:, columns].astype(jnp.float32)
        return (value * inverse * gain_ref[:, columns]).astype(jnp.bfloat16)

    send_ref[:, MAIN:] = weight_ref[...]
    last = normed(slice(MAIN, D))
    for k in range(3):
        columns = slice(k * TAIL, (k + 1) * TAIL)
        rows = jnp.concatenate([normed(columns), last], axis=0)
        select = jnp.concatenate(
            [pick_ref[:, :TOK], pick_ref[:, (k + 1) * TOK : (k + 2) * TOK]], axis=1
        )
        send_ref[:, columns] = dot_f32(select, rows).astype(jnp.bfloat16)


def front(query, key_value, prior_out, prior_lse, norm_gain, expert_ids, route_weight):
    vmem = pl.BlockSpec(memory_space=pltpu.VMEM)
    hbm = pl.BlockSpec(memory_space=pltpu.HBM)
    own = key_value[0]
    blocks = passed_along(own, 1), passed_along(own, 2)
    rows = EXPERTS * MSG_ROWS
    state = pl.pallas_call(
        front_kernel,
        out_shape=(
            jax.ShapeDtypeStruct((QUADS, 2 * LANES, LANES), jnp.bfloat16),
            jax.ShapeDtypeStruct((QUADS, LANES, 2 * LANES), jnp.float32),
            jax.ShapeDtypeStruct((4 * QUADS, LANES), jnp.float32),
            jax.ShapeDtypeStruct((4 * QUADS, LANES), jnp.float32),
            jax.ShapeDtypeStruct((rows, 4 * TOK), jnp.bfloat16),
            jax.ShapeDtypeStruct((rows, LANES), jnp.bfloat16),
        ),
        in_specs=[hbm] * 6,
        out_specs=(vmem,) * 6,
        scratch_shapes=[
            pltpu.VMEM((TOK, 2 * LANES), jnp.bfloat16),
            pltpu.VMEM((QUADS, 2 * LANES, LANES), jnp.bfloat16),
            pltpu.VMEM((HQ, TOK), jnp.float32),
            pltpu.VMEM((2, TOK), jnp.int32),
            pltpu.VMEM((2, TOK), jnp.bfloat16),
            pltpu.SemaphoreType.DMA((6,)),
        ],
        cost_estimate=pl.CostEstimate(
            flops=1_500_000_000, bytes_accessed=4_000_000, transcendentals=500_000
        ),
        compiler_params=pltpu.CompilerParams(vmem_limit_bytes=12 * 2**20),
        name="front",
    )(
        *(
            pltpu.with_memory_space_constraint(array, pltpu.HBM)
            for array in (
                query[0], own, prior_out[0], prior_lse[0].T, expert_ids[0].T, route_weight[0].T
            )
        )
    )
    return pl.pallas_call(
        back_kernel,
        out_shape=(
            jax.ShapeDtypeStruct((TOK, D), jnp.bfloat16),
            jax.ShapeDtypeStruct((rows, PAYLOAD), jnp.bfloat16),
        ),
        in_specs=[vmem] * 9,
        out_specs=(vmem, vmem),
        cost_estimate=pl.CostEstimate(
            flops=1_500_000_000, bytes_accessed=4_000_000, transcendentals=500_000
        ),
        compiler_params=pltpu.CompilerParams(vmem_limit_bytes=16 * 2**20),
        name="back",
    )(*blocks, *state, norm_gain[None, :])


def expert_kernel(got_ref, gate_ref, up_ref, out_ref, rows_ref, weight_ref):
    step_rows, step_slots = 16 * MSG_ROWS, 16 * CAP
    slot, source = iota((step_slots, step_rows), 0), iota((step_slots, step_rows), 1)
    rank, sender = lax.rem(slot, CAP), lax.div(slot, CAP) * MSG_ROWS
    main = as_bf16(source == sender + rank)
    tails = [
        as_bf16(
            ((rank == k) & (source == sender + 6)) | ((rank == 3 + k) & (source == sender + 7))
        )
        for k in range(3)
    ]
    tail = jnp.concatenate(tails, axis=1)
    for step in range(EXPERTS // 16):
        rows = slice(step * step_rows, (step + 1) * step_rows)
        slots = slice(step * step_slots, (step + 1) * step_slots)
        rows_ref[slots, :MAIN] = dot_f32(main, got_ref[rows, :MAIN]).astype(jnp.bfloat16)
        stacked = jnp.concatenate(
            [got_ref[rows, k * TAIL : (k + 1) * TAIL] for k in range(3)], axis=0
        )
        rows_ref[slots, MAIN:] = dot_f32(tail, stacked).astype(jnp.bfloat16)
        weight_ref[slots, :] = dot_f32(main, got_ref[rows, MAIN:])

    width = 256

    @pl.loop(0, FF // width)
    def _(tile):
        columns = pl.ds(pl.multiple_of(tile * width, width), width)
        gate = dot_f32(rows_ref[...], gate_ref[:, columns])
        up = dot_f32(rows_ref[...], up_ref[:, columns])
        weight = weight_ref[...]
        weight = jnp.concatenate([weight] * (width // LANES), axis=1)
        out_ref[:, columns] = (jax.nn.silu(gate) * up * weight).astype(jnp.bfloat16)


def expert_rows(got, w_gate, w_up):
    vmem = pl.BlockSpec(memory_space=pltpu.VMEM)
    return pl.pallas_call(
        expert_kernel,
        out_shape=jax.ShapeDtypeStruct((EXPERTS * CAP, FF), jnp.bfloat16),
        in_specs=[vmem] * 3,
        out_specs=vmem,
        scratch_shapes=[
            pltpu.VMEM((EXPERTS * CAP, D), jnp.bfloat16),
            pltpu.VMEM((EXPERTS * CAP, LANES), jnp.float32),
        ],
        cost_estimate=pl.CostEstimate(
            flops=2_600_000_000, bytes_accessed=9_000_000, transcendentals=300_000
        ),
        compiler_params=pltpu.CompilerParams(vmem_limit_bytes=20 * 2**20),
        name="expert_rows",
    )(got, w_gate, w_up)


def passed_along(block, distance):
    count = lax.axis_size("ctx")
    route = [((i - distance) % count, i) for i in range(count)]
    return lax.ppermute(block, "ctx", route)


def per_device(
    query, key_value, prior_out, prior_lse, norm_gain, w_gate, w_up, expert_ids, route_weight
):
    attended, payload = front(
        query, key_value, prior_out, prior_lse, norm_gain, expert_ids, route_weight
    )
    got = lax.all_to_all(
        payload.reshape(EXPERTS, MSG_ROWS, PAYLOAD), "exp", split_axis=0, concat_axis=0, tiled=True
    )
    hidden = expert_rows(got.reshape(EXPERTS * MSG_ROWS, PAYLOAD), w_gate[0], w_up[0])
    return attended[None], hidden[None, None]


def solution(mesh):
    placed = (
        P("exp", "ctx", None),
        P("exp", "ctx", None),
        P("exp", "ctx", None),
        P("exp", "ctx", None),
        P(),
        P("exp", None, None),
        P("exp", None, None),
        P("exp", "ctx", None),
        P("exp", "ctx", None),
    )
    return jax.shard_map(
        per_device,
        mesh=mesh,
        in_specs=placed,
        out_specs=(P("exp", "ctx", None), P("ctx", "exp", None, None)),
        check_vma=False,
    )
```

time: 107 us -> 95.4 us (0.89)
  Pallas kernels: 18.7 us -> 11.7 us
  waiting for transfers between devices: 17.4 us -> 14.2 us
    pallas_call x1 -> x2, Pallas kernels: 10.8 us -> 7.07 us  [the longest x1 3.87 us: front(): pl.pallas_call(back_kernel, out_shape=(jax.ShapeDtypeStruct((TOK, D), jnp...]
    pallas_call x1, Pallas kernels: 7.93 us -> 4.58 us  [expert_rows(): pl.pallas_call(expert_kernel, out_shape=jax.ShapeDtypeStruct((EXPERTS * C...]
    ppermute x2, waiting for transfers between devices: 17.4 us -> 14.2 us  [passed_along(): return lax.ppermute(block, 'ctx', route)]
  transfers between devices with their start and end apart: 2 -> 2, of which waited for: 2 -> 2; matrix products, arithmetic and copies ran while one was open for 0% -> 0% of each run, Pallas kernels for 0% -> 3%
where the time goes in v2:
time: 95.4 us; the launch traced here: 95.1 us
  blocking collectives  61.1 us (64%)
  waiting for transfers between devices  14.2 us (15%)
  Pallas kernels  11.7 us (12%)
  starting transfers between devices  7.43 us (8%)
    all_to_all x1, blocking collectives, per_device(): lax.all_to_all(payload.reshape(EXPERTS, MSG_ROWS, PAYLOAD), 'exp', split_...  61.1 us
    ppermute x2, waiting for transfers between devices, passed_along(): return lax.ppermute(block, 'ctx', route)  14.2 us
    ppermute x2, starting transfers between devices, passed_along(): return lax.ppermute(block, 'ctx', route)  7.43 us
    pallas_call x1, Pallas kernels, expert_rows(): pl.pallas_call(expert_kernel, out_shape=jax.ShapeDtypeStruct((EXPERTS * C...  4.58 us
    pallas_call x1, Pallas kernels, front(): pl.pallas_call(back_kernel, out_shape=(jax.ShapeDtypeStruct((TOK, D), jnp...  3.87 us
    pallas_call x1, Pallas kernels, front(): pl.pallas_call(front_kernel, out_shape=(jax.ShapeDtypeStruct((QUADS, 2 *...  3.2 us
  transfers between devices with their start and end apart: 2, of which 2 were waited for; matrix products, arithmetic and copies ran while one was open for 0% of the time, Pallas kernels for 3%

profile of v2, /device:TPU:16, one launch (start us, length us, event | category | flops | bytes accessed | tf_op | source)
XLA Modules:
  0.0 95.1 jit_solution(2080174159872008792)
XLA Ops:
  0.6 0.0 copy-start.2
  0.6 4.9 %collective-permute-start.1 = (bf16[128,256]{1,0:T(8,128)(2,1)}, bf16[128,256]{1,0:T(8,128)(2,1)S(1)}, u32[]{:S(2)}, u32[]{:S(2)}) collective-permute-start(bf16[128,256]{1,0:T(8,128)(2,1)} %bitcast.26), channel_id=1, source_target_pairs={{896,0},{960,64},{0,128},{64,192},{128,256},{192,320},{256,384},{3... | collective-permute-start | bytes 196616 | tf_op jit(solution)/shard_map/ppermute | solution.py:416
  5.6 2.5 %collective-permute-start = (bf16[128,256]{1,0:T(8,128)(2,1)}, bf16[128,256]{1,0:T(8,128)(2,1)S(1)}, u32[]{:S(2)}, u32[]{:S(2)}) collective-permute-start(bf16[128,256]{1,0:T(8,128)(2,1)} %bitcast.27), channel_id=1, source_target_pairs={{960,0},{0,64},{64,128},{128,192},{192,256},{256,320},{320,384},{3... | collective-permute-start | bytes 196616 | tf_op jit(solution)/shard_map/ppermute | solution.py:416
  8.1 3.2 %front.1 = (bf16[8,256,128]{2,1,0:T(8,128)(2,1)S(1)}, f32[8,128,256]{2,1,0:T(8,128)S(1)}, f32[32,128]{1,0:T(8,128)S(1)}, f32[32,128]{1,0:T(8,128)S(1)}, bf16[512...) custom-call(bf16[128,2048]{1,0:T(8,128)(2,1)} %bitcast.24, bf16[128,256]{1,0:T(8,128)(2,1)} %bitcast.28, ...), custom_call_target="tpu_custom_call" | custom-call | flops 1500000000 | bytes 4000000 | tf_op jit(solution)/shard_map/front/pallas_call | solution.py:311
  11.3 12.6 %collective-permute-done.1.kv2_ref = bf16[128,256]{1,0:T(8,128)(2,1)S(1)} collective-permute-done((bf16[128,256]{1,0:T(8,128)(2,1)}, bf16[128,256]{1,0:T(8,128)(2,1)S(1)}, u32[]{:S(2)}, u32[]{:S(2)}) %collective-permute-start.1) | collective-permute-done | bytes 65568 | tf_op jit(solution)/shard_map/ppermute | solution.py:416
  23.9 1.6 %collective-permute-done.kv1_ref = bf16[128,256]{1,0:T(8,128)(2,1)S(1)} collective-permute-done((bf16[128,256]{1,0:T(8,128)(2,1)}, bf16[128,256]{1,0:T(8,128)(2,1)S(1)}, u32[]{:S(2)}, u32[]{:S(2)}) %collective-permute-start) | collective-permute-done | bytes 65568 | tf_op jit(solution)/shard_map/ppermute | solution.py:416
  25.5 0.0 copy-done.2
  25.5 0.0 copy-start
  25.5 0.0 copy-start.1
  25.5 3.9 %back.1 = (bf16[128,2048]{1,0:T(8,128)(2,1)}, bf16[512,1664]{1,0:T(8,128)(2,1)S(1)}) custom-call(bf16[128,256]{1,0:T(8,128)(2,1)S(1)} %collective-permute-done.kv1_ref, bf16[128,256]{1,0:T(8,128)(2,1)S(1)} %collective-permute-done.1.kv2_ref, bf16[8,256,128]{2,1,0:T(8,128)(2,1)S(1)} %get-tuple-element.10.qs_ref, ...), custom_call_target="tpu_custom_call" | custom-call | flops 1500000000 | bytes 4000000 | tf_op jit(solution)/shard_map/back/pallas_call | solution.py:344
  29.4 61.1 %all_to_all.5 = bf16[64,8,1664]{2,1,0:T(8,128)(2,1)S(1)} all-to-all(bf16[64,8,1664]{2,1,0:T(8,128)(2,1)S(1)} %bitcast.19), channel_id=1, replica_groups=mesh['ctx'=16,'exp'=64] {'exp'}, dimensions={0} | all-to-all | bytes 3407872 | tf_op jit(solution)/shard_map/all_to_all | solution.py:425
  90.5 0.0 copy-done
  90.5 0.0 copy-done.1
  90.5 4.6 %expert_rows.1 = bf16[384,768]{1,0:T(8,128)(2,1)} custom-call(bf16[512,1664]{1,0:T(8,128)(2,1)S(1)} %bitcast.20, bf16[2048,768]{1,0:T(8,128)(2,1)S(1)} %bitcast.21, bf16[2048,768]{1,0:T(8,128)(2,1)S(1)} %bitcast.22), custom_call_target="tpu_custom_call" | custom-call | flops 2600000000 | bytes 9000000 | tf_op jit(solution)/shard_map/expert_rows/pallas_call | solution.py:396
Async XLA Ops:
  0.6 24.9 %copy-start.2 = (f32[2048]{0:T(1024)S(1)}, f32[2048]{0:T(1024)}, u32[]{:S(2)}) copy-start(f32[2048]{0:T(1024)} %param.13) | copy-start | bytes 24580
  0.6 23.3 %collective-permute-start.1 = (bf16[128,256]{1,0:T(8,128)(2,1)}, bf16[128,256]{1,0:T(8,128)(2,1)S(1)}, u32[]{:S(2)}, u32[]{:S(2)}) collective-permute-start(bf16[128,256]{1,0:T(8,128)(2,1)} %bitcast.26), channel_id=1, source_target_pairs={{896,0},{960,64},{0,128},{64,192},{128,256},{192,320},{256,384},{3... | collective-permute-start | bytes 196616 | tf_op jit(solution)/shard_map/ppermute | solution.py:416
  5.6 19.9 %collective-permute-start = (bf16[128,256]{1,0:T(8,128)(2,1)}, bf16[128,256]{1,0:T(8,128)(2,1)S(1)}, u32[]{:S(2)}, u32[]{:S(2)}) collective-permute-start(bf16[128,256]{1,0:T(8,128)(2,1)} %bitcast.27), channel_id=1, source_target_pairs={{960,0},{0,64},{64,128},{128,192},{192,256},{256,320},{320,384},{3... | collective-permute-start | bytes 196616 | tf_op jit(solution)/shard_map/ppermute | solution.py:416
  25.5 65.0 %copy-start = (bf16[1,2048,768]{2,1,0:T(8,128)(2,1)S(1)}, bf16[1,2048,768]{2,1,0:T(8,128)(2,1)}, u32[]{:S(2)}) copy-start(bf16[1,2048,768]{2,1,0:T(8,128)(2,1)} %param.14) | copy-start | bytes 9437188
  25.5 65.0 %copy-start.1 = (bf16[1,2048,768]{2,1,0:T(8,128)(2,1)S(1)}, bf16[1,2048,768]{2,1,0:T(8,128)(2,1)}, u32[]{:S(2)}) copy-start(bf16[1,2048,768]{2,1,0:T(8,128)(2,1)} %param.15) | copy-start | bytes 9437188

commit v3 on v2

--- a/solution.py
+++ b/solution.py
@@ -4,6 +4,7 @@
 from jax.experimental import pallas as pl
 from jax.experimental.pallas import tpu as pltpu
 from jax.sharding import PartitionSpec as P
+
 
 HQ = 32
 KVH = 2
@@ -18,7 +19,6 @@
 MSG_ROWS = 8
 MAIN = CAP * D // MSG_ROWS
 TAIL = D - MAIN
-PAYLOAD = MAIN + LANES
 LAST_LANES = (((1,), (1,)), ((), ()))
 PAIRS = KVH * 8
 QUADS = PAIRS // 2
@@ -85,7 +85,8 @@
     return jnp.concatenate([jnp.broadcast_to(row, (HD, row.shape[1])) for row in rows], axis=0)
 
 
-def slots(ids, weights, pick_ref, weight_ref):
+def slots_kernel(ids_ref, rw_ref, pick_ref, weight_ref):
+    ids, weights = ids_ref[...], rw_ref[...]
     experts = iota((EXPERTS, TOK), 0)
     chosen = [ids[j : j + 1, :] == experts for j in range(2)]
     named = chosen[0] | chosen[1]
@@ -117,15 +118,13 @@
 
 
 def front_kernel(
-    q_hbm, kv_hbm, prior_hbm, lse_hbm, ids_hbm, rw_hbm,
-    qs_ref, mix_ref, top_ref, sum_ref, pick_ref, weight_ref,
-    kv_ref, prior_ref, lse_ref, ids_ref, rw_ref, sems,
+    q_hbm, kv_hbm, prior_hbm, lse_hbm,
+    qs_ref, mix_ref, top_ref, sum_ref,
+    kv_ref, prior_ref, lse_ref, sems,
 ):
     copies = [
         pltpu.make_async_copy(kv_hbm, kv_ref, sems.at[0]),
         pltpu.make_async_copy(lse_hbm, lse_ref, sems.at[1]),
-        pltpu.make_async_copy(ids_hbm, ids_ref, sems.at[2]),
-        pltpu.make_async_copy(rw_hbm, rw_ref, sems.at[3]),
     ]
     for copy in copies:
         copy.start()
@@ -136,16 +135,15 @@
                 rows, columns = slice(half * HALF, (half + 1) * HALF), slice(pair * LANES, (pair + 1) * LANES)
                 target = slice(half * LANES + i * HALF, half * LANES + (i + 1) * HALF)
                 moves.append(
-                    pltpu.make_async_copy(q_hbm.at[rows, columns], qs_ref.at[quad, target, :], sems.at[4])
+                    pltpu.make_async_copy(q_hbm.at[rows, columns], qs_ref.at[quad, target, :], sems.at[2])
                 )
                 moves.append(
-                    pltpu.make_async_copy(prior_hbm.at[rows, columns], prior_ref.at[quad, target, :], sems.at[5])
+                    pltpu.make_async_copy(prior_hbm.at[rows, columns], prior_ref.at[quad, target, :], sems.at[3])
                 )
     for move in moves:
         move.start()
     for copy in copies:
         copy.wait()
-    slots(ids_ref[...], rw_ref[...], pick_ref, weight_ref)
     keys, values = lay([kv_ref[:HALF, :], kv_ref[HALF:, :]])
     eye = unit()
     low = iota((1, LANES), 1) < HALF
@@ -201,7 +199,7 @@
 
 
 def back_kernel(
-    kv1_ref, kv2_ref, qs_ref, mix_ref, top_ref, sum_ref, pick_ref, weight_ref, gain_ref,
+    kv1_ref, kv2_ref, qs_ref, mix_ref, top_ref, sum_ref, pick_ref, gain_ref,
     out_ref, send_ref,
 ):
     block = lax.axis_index("ctx")
@@ -291,7 +289,6 @@
         value = out_ref[:, columns].astype(jnp.float32)
         return (value * inverse * gain_ref[:, columns]).astype(jnp.bfloat16)
 
-    send_ref[:, MAIN:] = weight_ref[...]
     last = normed(slice(MAIN, D))
     for k in range(3):
         columns = slice(k * TAIL, (k + 1) * TAIL)
@@ -306,27 +303,59 @@
     vmem = pl.BlockSpec(memory_space=pltpu.VMEM)
     hbm = pl.BlockSpec(memory_space=pltpu.HBM)
     own = key_value[0]
-    blocks = passed_along(own, 1), passed_along(own, 2)
+    first = passed_along(own, 1)
+    second = passed_along(own, 2)
     rows = EXPERTS * MSG_ROWS
-    state = pl.pallas_call(
+    pick, weights = pl.pallas_call(
+        slots_kernel,
+        out_shape=(
+            jax.ShapeDtypeStruct((rows, 4 * TOK), jnp.bfloat16),
+            jax.ShapeDtypeStruct((rows, LANES), jnp.bfloat16),
+        ),
+        in_specs=[vmem] * 2,
+        out_specs=(vmem,) * 2,
+        cost_estimate=pl.CostEstimate(
+            flops=100_000_000, bytes_accessed=700_000, transcendentals=0
+        ),
+        name="slots",
+    )(expert_ids[0].T, route_weight[0].T)
+    arrived = to_experts(weights)
+    state = front_call(query, own, prior_out, prior_lse)
+    attended, payload = pl.pallas_call(
+        back_kernel,
+        out_shape=(
+            jax.ShapeDtypeStruct((TOK, D), jnp.bfloat16),
+            jax.ShapeDtypeStruct((rows, MAIN), jnp.bfloat16),
+        ),
+        in_specs=[vmem] * 8,
+        out_specs=(vmem, vmem),
+        cost_estimate=pl.CostEstimate(
+            flops=1_500_000_000, bytes_accessed=4_000_000, transcendentals=500_000
+        ),
+        compiler_params=pltpu.CompilerParams(vmem_limit_bytes=16 * 2**20),
+        name="back",
+    )(first, second, *state, pick, norm_gain[None, :])
+    return attended, payload, arrived
+
+
+def front_call(query, own, prior_out, prior_lse):
+    vmem = pl.BlockSpec(memory_space=pltpu.VMEM)
+    hbm = pl.BlockSpec(memory_space=pltpu.HBM)
+    return pl.pallas_call(
         front_kernel,
         out_shape=(
             jax.ShapeDtypeStruct((QUADS, 2 * LANES, LANES), jnp.bfloat16),
             jax.ShapeDtypeStruct((QUADS, LANES, 2 * LANES), jnp.float32),
             jax.ShapeDtypeStruct((4 * QUADS, LANES), jnp.float32),
             jax.ShapeDtypeStruct((4 * QUADS, LANES), jnp.float32),
-            jax.ShapeDtypeStruct((rows, 4 * TOK), jnp.bfloat16),
-            jax.ShapeDtypeStruct((rows, LANES), jnp.bfloat16),
-        ),
-        in_specs=[hbm] * 6,
-        out_specs=(vmem,) * 6,
+        ),
+        in_specs=[hbm] * 4,
+        out_specs=(vmem,) * 4,
         scratch_shapes=[
             pltpu.VMEM((TOK, 2 * LANES), jnp.bfloat16),
             pltpu.VMEM((QUADS, 2 * LANES, LANES), jnp.bfloat16),
             pltpu.VMEM((HQ, TOK), jnp.float32),
-            pltpu.VMEM((2, TOK), jnp.int32),
-            pltpu.VMEM((2, TOK), jnp.bfloat16),
-            pltpu.SemaphoreType.DMA((6,)),
+            pltpu.SemaphoreType.DMA((4,)),
         ],
         cost_estimate=pl.CostEstimate(
             flops=1_500_000_000, bytes_accessed=4_000_000, transcendentals=500_000
@@ -337,27 +366,23 @@
         *(
             pltpu.with_memory_space_constraint(array, pltpu.HBM)
             for array in (
-                query[0], own, prior_out[0], prior_lse[0].T, expert_ids[0].T, route_weight[0].T
+                query[0], own, prior_out[0], prior_lse[0].T
             )
         )
     )
-    return pl.pallas_call(
-        back_kernel,
-        out_shape=(
-            jax.ShapeDtypeStruct((TOK, D), jnp.bfloat16),
-            jax.ShapeDtypeStruct((rows, PAYLOAD), jnp.bfloat16),
-        ),
-        in_specs=[vmem] * 9,
-        out_specs=(vmem, vmem),
-        cost_estimate=pl.CostEstimate(
-            flops=1_500_000_000, bytes_accessed=4_000_000, transcendentals=500_000
-        ),
-        compiler_params=pltpu.CompilerParams(vmem_limit_bytes=16 * 2**20),
-        name="back",
-    )(*blocks, *state, norm_gain[None, :])
-
-
-def expert_kernel(got_ref, gate_ref, up_ref, out_ref, rows_ref, weight_ref):
+
+
+def to_experts(rows):
+    parts = rows.reshape(EXPERTS, MSG_ROWS, rows.shape[-1])
+    parts = lax.all_to_all(parts, "exp", split_axis=0, concat_axis=0, tiled=True)
+    return parts.reshape(rows.shape)
+
+
+def expert_kernel(
+    got_ref, sent_ref, gate_ref, up_hbm, out_ref, rows_ref, weight_ref, up_ref, gated_ref, sem
+):
+    copy = pltpu.make_async_copy(up_hbm, up_ref, sem)
+    copy.start()
     step_rows, step_slots = 16 * MSG_ROWS, 16 * CAP
     slot, source = iota((step_slots, step_rows), 0), iota((step_slots, step_rows), 1)
     rank, sender = lax.rem(slot, CAP), lax.div(slot, CAP) * MSG_ROWS
@@ -377,37 +402,48 @@
             [got_ref[rows, k * TAIL : (k + 1) * TAIL] for k in range(3)], axis=0
         )
         rows_ref[slots, MAIN:] = dot_f32(tail, stacked).astype(jnp.bfloat16)
-        weight_ref[slots, :] = dot_f32(main, got_ref[rows, MAIN:])
+        weight_ref[slots, :] = dot_f32(main, sent_ref[rows, :])
 
     width = 256
+
+    def columns_of(tile):
+        return pl.ds(pl.multiple_of(tile * width, width), width)
 
     @pl.loop(0, FF // width)
     def _(tile):
-        columns = pl.ds(pl.multiple_of(tile * width, width), width)
-        gate = dot_f32(rows_ref[...], gate_ref[:, columns])
+        columns = columns_of(tile)
+        weight = jnp.concatenate([weight_ref[...]] * (width // LANES), axis=1)
+        gated_ref[:, columns] = jax.nn.silu(dot_f32(rows_ref[...], gate_ref[:, columns])) * weight
+
+    copy.wait()
+
+    @pl.loop(0, FF // width)
+    def _(tile):
+        columns = columns_of(tile)
         up = dot_f32(rows_ref[...], up_ref[:, columns])
-        weight = weight_ref[...]
-        weight = jnp.concatenate([weight] * (width // LANES), axis=1)
-        out_ref[:, columns] = (jax.nn.silu(gate) * up * weight).astype(jnp.bfloat16)
-
-
-def expert_rows(got, w_gate, w_up):
+        out_ref[:, columns] = (gated_ref[:, columns] * up).astype(jnp.bfloat16)
+
+
+def expert_rows(got, sent, w_gate, w_up):
     vmem = pl.BlockSpec(memory_space=pltpu.VMEM)
     return pl.pallas_call(
         expert_kernel,
         out_shape=jax.ShapeDtypeStruct((EXPERTS * CAP, FF), jnp.bfloat16),
-        in_specs=[vmem] * 3,
+        in_specs=[vmem, vmem, vmem, pl.BlockSpec(memory_space=pltpu.HBM)],
         out_specs=vmem,
         scratch_shapes=[
             pltpu.VMEM((EXPERTS * CAP, D), jnp.bfloat16),
             pltpu.VMEM((EXPERTS * CAP, LANES), jnp.float32),
+            pltpu.VMEM((D, FF), jnp.bfloat16),
+            pltpu.VMEM((EXPERTS * CAP, FF), jnp.float32),
+            pltpu.SemaphoreType.DMA,
         ],
         cost_estimate=pl.CostEstimate(
             flops=2_600_000_000, bytes_accessed=9_000_000, transcendentals=300_000
         ),
         compiler_params=pltpu.CompilerParams(vmem_limit_bytes=20 * 2**20),
         name="expert_rows",
-    )(got, w_gate, w_up)
+    )(got, sent, w_gate, pltpu.with_memory_space_constraint(w_up, pltpu.HBM))
 
 
 def passed_along(block, distance):
@@ -419,13 +455,10 @@
 def per_device(
     query, key_value, prior_out, prior_lse, norm_gain, w_gate, w_up, expert_ids, route_weight
 ):
-    attended, payload = front(
+    attended, payload, weights = front(
         query, key_value, prior_out, prior_lse, norm_gain, expert_ids, route_weight
     )
-    got = lax.all_to_all(
-        payload.reshape(EXPERTS, MSG_ROWS, PAYLOAD), "exp", split_axis=0, concat_axis=0, tiled=True
-    )
-    hidden = expert_rows(got.reshape(EXPERTS * MSG_ROWS, PAYLOAD), w_gate[0], w_up[0])
+    hidden = expert_rows(to_experts(payload), weights, w_gate[0], w_up[0])
     return attended[None], hidden[None, None]
 
 

time: 95.4 us -> 107 us (1.12)
  starting transfers between devices: 7.43 us -> 21.1 us
  blocking collectives: 61.1 us -> 58.6 us
  Pallas kernels: 11.7 us -> 13.8 us
  waiting for transfers between devices: 14.2 us -> 12.1 us
    all_to_all x0 -> x1, starting transfers between devices: none -> 17.2 us  [to_experts(): lax.all_to_all(parts, 'exp', split_axis=0, concat_axis=0, tiled=True)]
    ppermute x2, starting transfers between devices: 7.43 us -> 3.85 us  [passed_along(): return lax.ppermute(block, 'ctx', route)]
    all_to_all x1, blocking collectives: 61.1 us -> 58.6 us  [to_experts(): lax.all_to_all(parts, 'exp', split_axis=0, concat_axis=0, tiled=True)]
    ppermute x2, waiting for transfers between devices: 14.2 us -> 12.1 us  [passed_along(): return lax.ppermute(block, 'ctx', route)]
    pallas_call x1 -> x2, Pallas kernels: 3.2 us -> 4.8 us  [the longest x1 2.64 us: front_call(): pl.pallas_call(front_kernel, out_shape=(jax.ShapeDtypeStruct((QUADS, 2 *...]
  transfers between devices with their start and end apart: 2 -> 3, of which waited for: 2 -> 2; matrix products, arithmetic and copies ran while one was open for 0% -> 0% of each run, Pallas kernels for 3% -> 6%
where the time goes in v3:
time: 107 us; the launch traced here: 106 us
  blocking collectives  58.6 us (55%)
  starting transfers between devices  21.1 us (20%)
  Pallas kernels  13.8 us (13%)
  waiting for transfers between devices  12.1 us (11%)
    all_to_all x1, blocking collectives, to_experts(): lax.all_to_all(parts, 'exp', split_axis=0, concat_axis=0, tiled=True)  58.6 us
    all_to_all x1, starting transfers between devices, to_experts(): lax.all_to_all(parts, 'exp', split_axis=0, concat_axis=0, tiled=True)  17.2 us
    ppermute x2, waiting for transfers between devices, passed_along(): return lax.ppermute(block, 'ctx', route)  12.1 us
    pallas_call x1, Pallas kernels, expert_rows(): pl.pallas_call(expert_kernel, out_shape=jax.ShapeDtypeStruct((EXPERTS * C...  5.1 us
    pallas_call x1, Pallas kernels, front(): pl.pallas_call(back_kernel, out_shape=(jax.ShapeDtypeStruct((TOK, D), jnp...  3.88 us
    ppermute x2, starting transfers between devices, passed_along(): return lax.ppermute(block, 'ctx', route)  3.85 us
    pallas_call x1, Pallas kernels, front_call(): pl.pallas_call(front_kernel, out_shape=(jax.ShapeDtypeStruct((QUADS, 2 *...  2.64 us
    pallas_call x1, Pallas kernels, front(): pl.pallas_call(slots_kernel, out_shape=(jax.ShapeDtypeStruct((rows, 4 * T...  2.16 us
  transfers between devices with their start and end apart: 3, of which 2 were waited for; matrix products, arithmetic and copies ran while one was open for 0% of the time, Pallas kernels for 6%

profile of v3, /device:TPU:16, one launch (start us, length us, event | category | flops | bytes accessed | tf_op | source)
XLA Modules:
  0.0 106.2 jit_solution(16959967162080084451)
XLA Ops:
  0.6 0.0 copy-start.1
  0.6 2.2 %slots.1 = (bf16[512,512]{1,0:T(8,128)(2,1)}, bf16[512,128]{1,0:T(8,128)(2,1)}) custom-call(s32[2,128]{1,0:T(2,128)} %bitcast.34, bf16[2,128]{1,0:T(2,128)(2,1)} %bitcast.35), custom_call_target="tpu_custom_call" | custom-call | flops 100000000 | bytes 700000 | tf_op jit(solution)/shard_map/slots/pallas_call | solution.py:309
  2.8 0.0 copy-start.2
  2.8 17.2 %all-to-all-start.1 = ((bf16[64,8,128]{2,1,0:T(8,128)(2,1)}), bf16[64,8,128]{2,1,0:T(8,128)(2,1)S(1)}, u32[]{:S(2)}, u32[]{:S(2)}) async-start(bf16[64,8,128]{2,1,0:T(8,128)(2,1)} %bitcast.26), calls=%async_computation.1 | async-start | bytes 262144 | tf_op jit(solution)/shard_map/all_to_all | solution.py:377
  20.0 1.9 %collective-permute-start.1 = (bf16[128,256]{1,0:T(8,128)(2,1)}, bf16[128,256]{1,0:T(8,128)(2,1)S(1)}, u32[]{:S(2)}, u32[]{:S(2)}) collective-permute-start(bf16[128,256]{1,0:T(8,128)(2,1)} %bitcast.30), channel_id=1, source_target_pairs={{896,0},{960,64},{0,128},{64,192},{128,256},{192,320},{256,384},{3... | collective-permute-start | bytes 196616 | tf_op jit(solution)/shard_map/ppermute | solution.py:452
  22.0 1.9 %collective-permute-start = (bf16[128,256]{1,0:T(8,128)(2,1)}, bf16[128,256]{1,0:T(8,128)(2,1)S(1)}, u32[]{:S(2)}, u32[]{:S(2)}) collective-permute-start(bf16[128,256]{1,0:T(8,128)(2,1)} %bitcast.31), channel_id=1, source_target_pairs={{960,0},{0,64},{64,128},{128,192},{192,256},{256,320},{320,384},{3... | collective-permute-start | bytes 196616 | tf_op jit(solution)/shard_map/ppermute | solution.py:452
  23.9 2.6 %front.1 = (bf16[8,256,128]{2,1,0:T(8,128)(2,1)S(1)}, f32[8,128,256]{2,1,0:T(8,128)S(1)}, f32[32,128]{1,0:T(8,128)S(1)}, f32[32,128]{1,0:T(8,128)S(1)}) custom-call(bf16[128,2048]{1,0:T(8,128)(2,1)} %bitcast.28, bf16[128,256]{1,0:T(8,128)(2,1)} %bitcast.32, bf16[128,2048]{1,0:T(8,128)(2,1)} %bitcast.29, f32[32,128]{1,0:T(8,128)} %bitcast.33), custom_call_target="tpu_custom_call" | custom-call | flops 1500000000 | bytes 4000000 | tf_op jit(solution)/shard_map/front/pallas_call | solution.py:344
  26.6 10.4 %collective-permute-done.1.kv2_ref = bf16[128,256]{1,0:T(8,128)(2,1)S(1)} collective-permute-done((bf16[128,256]{1,0:T(8,128)(2,1)}, bf16[128,256]{1,0:T(8,128)(2,1)S(1)}, u32[]{:S(2)}, u32[]{:S(2)}) %collective-permute-start.1) | collective-permute-done | bytes 65568 | tf_op jit(solution)/shard_map/ppermute | solution.py:452
  37.0 1.7 %collective-permute-done.kv1_ref = bf16[128,256]{1,0:T(8,128)(2,1)S(1)} collective-permute-done((bf16[128,256]{1,0:T(8,128)(2,1)}, bf16[128,256]{1,0:T(8,128)(2,1)S(1)}, u32[]{:S(2)}, u32[]{:S(2)}) %collective-permute-start) | collective-permute-done | bytes 65568 | tf_op jit(solution)/shard_map/ppermute | solution.py:452
  38.7 0.0 copy-done.1
  38.7 0.0 copy-done.2
  38.7 3.9 %back.1 = (bf16[128,2048]{1,0:T(8,128)(2,1)}, bf16[512,1536]{1,0:T(8,128)(2,1)S(1)}) custom-call(bf16[128,256]{1,0:T(8,128)(2,1)S(1)} %collective-permute-done.kv1_ref, bf16[128,256]{1,0:T(8,128)(2,1)S(1)} %collective-permute-done.1.kv2_ref, bf16[8,256,128]{2,1,0:T(8,128)(2,1)S(1)} %get-tuple-element.10.qs_ref, ...), custom_call_target="tpu_custom_call" | custom-call | flops 1500000000 | bytes 4000000 | tf_op jit(solution)/shard_map/back/pallas_call | solution.py:324
  42.5 0.0 all-to-all-done.1
  42.5 0.0 copy-start
  42.5 58.6 %all_to_all.10 = bf16[64,8,1536]{2,1,0:T(8,128)(2,1)S(1)} all-to-all(bf16[64,8,1536]{2,1,0:T(8,128)(2,1)S(1)} %bitcast.21), channel_id=1, replica_groups=mesh['ctx'=16,'exp'=64] {'exp'}, dimensions={0} | all-to-all | bytes 3145728 | tf_op jit(solution)/shard_map/all_to_all | solution.py:377
  101.1 0.0 copy-done
  101.1 5.1 %expert_rows.1 = bf16[384,768]{1,0:T(8,128)(2,1)} custom-call(bf16[512,1536]{1,0:T(8,128)(2,1)S(1)} %bitcast.22, bf16[512,128]{1,0:T(8,128)(2,1)S(1)} %bitcast.23, bf16[2048,768]{1,0:T(8,128)(2,1)S(1)} %bitcast.24, bf16[2048,768]{1,0:T(8,128)(2,1)} %bitcast.27), custom_call_target="tpu_custom_call" | custom-call | flops 2600000000 | bytes 9000000 | tf_op jit(solution)/shard_map/expert_rows/pallas_call | solution.py:429
Async XLA Ops:
  0.6 38.0 %copy-start.1 = (f32[2048]{0:T(1024)S(1)}, f32[2048]{0:T(1024)}, u32[]{:S(2)}) copy-start(f32[2048]{0:T(1024)} %param.13) | copy-start | bytes 24580
  2.8 35.9 %copy-start.2 = (bf16[512,512]{1,0:T(8,128)(2,1)S(1)}, bf16[512,512]{1,0:T(8,128)(2,1)}, u32[]{:S(2)}) copy-start(bf16[512,512]{1,0:T(8,128)(2,1)} %get-tuple-element.14.pick_ref) | copy-start | bytes 1572868
  2.8 39.7 %all-to-all-start.1 = ((bf16[64,8,128]{2,1,0:T(8,128)(2,1)}), bf16[64,8,128]{2,1,0:T(8,128)(2,1)S(1)}, u32[]{:S(2)}, u32[]{:S(2)}) async-start(bf16[64,8,128]{2,1,0:T(8,128)(2,1)} %bitcast.26), calls=%async_computation.1 | async-start | bytes 262144 | tf_op jit(solution)/shard_map/all_to_all | solution.py:377
  20.0 17.0 %collective-permute-start.1 = (bf16[128,256]{1,0:T(8,128)(2,1)}, bf16[128,256]{1,0:T(8,128)(2,1)S(1)}, u32[]{:S(2)}, u32[]{:S(2)}) collective-permute-start(bf16[128,256]{1,0:T(8,128)(2,1)} %bitcast.30), channel_id=1, source_target_pairs={{896,0},{960,64},{0,128},{64,192},{128,256},{192,320},{256,384},{3... | collective-permute-start | bytes 196616 | tf_op jit(solution)/shard_map/ppermute | solution.py:452
  22.0 16.7 %collective-permute-start = (bf16[128,256]{1,0:T(8,128)(2,1)}, bf16[128,256]{1,0:T(8,128)(2,1)S(1)}, u32[]{:S(2)}, u32[]{:S(2)}) collective-permute-start(bf16[128,256]{1,0:T(8,128)(2,1)} %bitcast.31), channel_id=1, source_target_pairs={{960,0},{0,64},{64,128},{128,192},{192,256},{256,320},{320,384},{3... | collective-permute-start | bytes 196616 | tf_op jit(solution)/shard_map/ppermute | solution.py:452
  42.5 58.6 %copy-start = (bf16[1,2048,768]{2,1,0:T(8,128)(2,1)S(1)}, bf16[1,2048,768]{2,1,0:T(8,128)(2,1)}, u32[]{:S(2)}) copy-start(bf16[1,2048,768]{2,1,0:T(8,128)(2,1)} %param.14) | copy-start | bytes 9437188
